TPU v7x, 32 devices: a whole 2x2x4 slice. The times are simulated.
32 devices in a mesh: gx: 4 (over x, core), gy: 8 (over z, y).
Axes of the slice: x: 2, y: 2, z: 4, core: 2. Of those that a mesh axis runs over, the one named last changes fastest.
Arguments:
- hidden: bfloat16 [8, 512, 1280], P('gy', 'gx'), may hold values from -6 to 6
- lengths: int32 [8], P('gy'), may hold values from 4 to 16384, as said below
- sink_kv: bfloat16 [8, 2, 4, 1024], P('gy', None, None, 'gx'), may hold values from -12 to 12
- kv_cycle: bfloat16 [8, 2, 4608, 1024], P('gy', None, None, 'gx'), may hold values from -12 to 12
- w_qkv: bfloat16 [1280, 3, 1024], P('gy', None, 'gx'), may hold values from -0.15625 to 0.15625
- s_qk: float32 [1024], P('gx'), may hold values from 0.5 to 16
- w_out: bfloat16 [1024, 1280], P('gx', 'gy'), may hold values from -0.1875 to 0.1875
- alpha_attn: float32 [1280], replicated, may hold values from 0.05 to 0.8
- w_up: bfloat16 [1280, 5120], P('gy', 'gx'), may hold values from -0.15625 to 0.15625
- w_gate: bfloat16 [1280, 5120], P('gy', 'gx'), may hold values from -0.15625 to 0.15625
- s_up: float32 [5120], P('gx'), may hold values from 0.5 to 2
- s_gate: float32 [5120], P('gx'), may hold values from 0.5 to 2
- w_down: bfloat16 [5120, 1280], P('gx', 'gy'), may hold values from -0.078125 to 0.078125
- alpha_mlp: float32 [1280], replicated, may hold values from 0.05 to 0.8
Outputs:
- new_hidden: bfloat16 [8, 512, 1280], P('gy', 'gx')
- new_cycle: bfloat16 [8, 2, 4608, 1024], P('gy', None, None, 'gx')
Inputs may be any that keep to these rules, and one draw needn't show every extreme that they name: `lengths`: exactly 2 requests, chosen by the seed, have 16384 cached positions; the others have fewer than 256.
All inputs are finite; a program needn't handle non-finite values.
Results may differ from a plain program's by a relative error of at most 0.012.
The roundings to bfloat16 on the way count: a program that leaves them out, or rounds other values in their place, can miss the bound.
Values may be sent and summed in bfloat16 or wider, within the bound.
No kernel may reach another device: no remote copies, remote signals or barrier semaphores. Data moves between devices by JAX's collectives and lax.ppermute only.
A program may use at most 64 MiB of HBM per device.

v0:
```python
import functools
import math

import jax
import jax.numpy as jnp
from jax import lax
from jax.experimental import pallas as pl
from jax.experimental.pallas import tpu as pltpu
from jax.sharding import PartitionSpec as P


HD = 64
SINK = 4
WINDOW = 4096
SHORT_KEYS = 768
CHUNK = 512
NEG = -1e30
FIXED = 4
VMEM = pl.BlockSpec(memory_space=pltpu.VMEM)
SMEM = pl.BlockSpec(memory_space=pltpu.SMEM)
ANY = pl.BlockSpec(memory_space=pl.ANY)
PARAMS = pltpu.CompilerParams(vmem_limit_bytes=56 << 20)


def rms_unit(values):
    return values * lax.rsqrt(jnp.mean(values * values, axis=-1, keepdims=True) + 1e-06)


class Layout:
    def __init__(self, gx, gy):
        self.plain = (gx, gy) != (4, 8)
        self.nx = gx // 2
        self.ny = self.nx
        self.nz = gy // self.ny
        mine_x, mine_y = lax.axis_index("gx"), lax.axis_index("gy")
        self.x, self.c = mine_x // 2, mine_x % 2
        self.z, self.y = mine_y // self.ny, mine_y % self.ny

    def from_z(self, value):
        pairs = [
            (z * self.ny + y, (z - 1) % self.nz * self.ny + y)
            for z in range(self.nz)
            for y in range(self.ny)
        ]
        return lax.ppermute(value, "gy", pairs)

    def from_y(self, value):
        pairs = [
            (z * self.ny + y, z * self.ny + (y - 1) % self.ny)
            for z in range(self.nz)
            for y in range(self.ny)
        ]
        return lax.ppermute(value, "gy", pairs)

    def to_x(self, value, step):
        pairs = [
            (x * 2 + c, (x + step) % self.nx * 2 + c) for x in range(self.nx) for c in range(2)
        ]
        return lax.ppermute(value, "gx", pairs)

    def swap_core(self, value):
        pairs = [(x * 2 + c, x * 2 + 1 - c) for x in range(self.nx) for c in range(2)]
        return lax.ppermute(value, "gx", pairs)

    def blocks(self):
        if self.plain:
            return [jnp.int32(0)]
        return [
            (self.z + k) % self.nz * self.ny + (self.y + j) % self.ny
            for k in range(self.nz)
            for j in range(self.ny)
        ]

    def gather(self, shard):
        if self.plain:
            return [(lax.all_gather(shard, "gy", axis=shard.ndim - 2, tiled=True), ())]
        pieces = []
        held = shard
        for k in range(self.nz):
            if k:
                held = self.from_z(held)
            side = held
            for j in range(self.ny):
                if j:
                    side = self.from_y(side)
                pieces.append((side, ()))
        return pieces

    def gather_y_first(self, shard):
        if self.plain:
            return self.gather(shard)
        held = [shard]
        for _ in range(1, self.ny):
            held.append(self.from_y(held[-1]))
        held = jnp.stack(held)
        pieces = []
        for k in range(self.nz):
            if k:
                held = self.from_z(held)
            pieces += [(held, (j,)) for j in range(self.ny)]
        return pieces

    def core_sum(self, halves):
        kept, sent = halves
        return kept.astype(jnp.float32) + self.swap_core(sent).astype(jnp.float32)


def pieces_of(pieces):
    arrays, spots = [], []
    for array, index in pieces:
        known = [n for n, other in enumerate(arrays) if other is array]
        if not known:
            arrays.append(array)
        spots.append((known[0] if known else len(arrays) - 1, index))
    return arrays, tuple(spots)


def place(scalars, refs, spots, held, plane=(), lane=0):
    for n, (number, index) in enumerate(spots):
        value = refs[number][index + plane]
        rows, lanes = value.shape
        at = pl.multiple_of(scalars[FIXED + n] * rows, 16)
        held[pl.ds(at, rows), lane : lane + lanes] = value


def split_rows(value, kept_ref, sent_ref, own_rows):
    for d in range(value.shape[0] // (2 * own_rows)):
        at = slice(d * own_rows, (d + 1) * own_rows)
        kept_ref[at, :] = value[2 * d * own_rows : (2 * d + 1) * own_rows]
        sent_ref[at, :] = value[(2 * d + 1) * own_rows : (2 * d + 2) * own_rows]


def stage_kernel(source, target):
    target[...] = source[...]


def qkv_kernel(spots, count, blocks, own_rows, scalars, scale_ref, cycle_in, *rest):
    pieces, row_refs = rest[:count], rest[count : count + blocks]
    query_ref, cycle_ref, window, fresh, held, sems = rest[count + blocks :]
    del cycle_in
    length, x, c, nx = scalars[0], scalars[1], scalars[2], scalars[3]
    new_count, local_cols = query_ref.shape
    cycle_size = cycle_ref.shape[1]
    span = window.shape[1]
    start = lax.rem(length - SINK, cycle_size)
    base = jnp.minimum(start // 16 * 16, cycle_size - span)
    base = pl.multiple_of(base, 16)
    loads = [
        pltpu.make_async_copy(cycle_ref.at[i, pl.ds(base, span), :], window.at[i], sems.at[i])
        for i in range(2)
    ]
    for load in loads:
        load.start()
    rows = jnp.concatenate([ref[...] for ref in row_refs], axis=0)
    lane_head = lax.broadcasted_iota(jnp.int32, (1, local_cols), 1) // HD

    def unit(values):
        squares = values * values
        total = jnp.zeros_like(values)
        for head in range(local_cols // HD):
            picked = lane_head == head
            part = jnp.sum(jnp.where(picked, squares, 0.0), axis=-1, keepdims=True)
            total = jnp.where(picked, part, total)
        return values * lax.rsqrt(total + 1e-06) * scale_ref[...]

    def project(which):
        place(scalars, pieces, spots, held.at[which], (which,))
        return jnp.dot(rows, held[which], preferred_element_type=jnp.float32)

    queries = unit(project(0)).astype(jnp.bfloat16)
    query_ref[...] = (queries.astype(jnp.float32) * math.sqrt(HD)).astype(jnp.bfloat16)
    fresh[0] = unit(project(1)).astype(jnp.bfloat16)
    fresh[1] = project(2).astype(jnp.bfloat16)
    row = lax.broadcasted_iota(jnp.int32, (1, new_count), 1)
    block, inside = row // own_rows, row % own_rows
    from_x = lax.rem(x - block // 2 + nx, nx)
    from_c = jnp.where(block % 2 == 1, 1 - c, c)
    token = (from_x * 2 + from_c) * own_rows + inside
    target = token + (start - base)
    slot = lax.broadcasted_iota(jnp.int32, (span, 1), 0)
    pick = (slot == target).astype(jnp.float32).astype(jnp.bfloat16)
    offset = slot - (start - base)
    replaced = (offset >= 0) & (offset < new_count)
    stores = []
    for i in range(2):
        loads[i].wait()
        moved = jnp.dot(pick, fresh[i], preferred_element_type=jnp.float32)
        window[i] = jnp.where(replaced, moved, window[i].astype(jnp.float32)).astype(jnp.bfloat16)
        store = pltpu.make_async_copy(
            window.at[i], cycle_ref.at[i, pl.ds(base, span), :], sems.at[i]
        )
        store.start()
        stores.append(store)
    for store in stores:
        store.wait()


def attention_kernel(own_rows, scalars, query_ref, cycle_ref, sink_ref, out_ref, scores, bias):
    length, x, c, nx = scalars[0], scalars[1], scalars[2], scalars[3]
    new_count, lanes = query_ref.shape
    cycle_size = cycle_ref.shape[1]
    lane_head = lax.broadcasted_iota(jnp.int32, (1, lanes), 1) // HD
    sink_lane = lax.broadcasted_iota(jnp.int32, (1, sink_ref.shape[1]), 1)
    sink_bias = jnp.where(sink_lane < SINK, 0.0, NEG)
    contract = (((1,), (1,)), ((), ()))

    def run(keys):
        sizes = [min(CHUNK, keys - at) for at in range(0, keys, CHUNK)]
        starts = [CHUNK * n for n in range(len(sizes))]

        def tile(i, _):
            from_x = lax.rem(x - i // 2 + nx, nx)
            from_c = jnp.where(i % 2 == 1, 1 - c, c)
            first = (from_x * 2 + from_c) * own_rows
            at = pl.multiple_of(i * own_rows, own_rows)
            queries = query_ref[pl.ds(at, own_rows), :]
            moment = first + lax.broadcasted_iota(jnp.int32, (own_rows, 1), 0)
            for begin, size in zip(starts, sizes):
                slot = begin + lax.broadcasted_iota(jnp.int32, (1, size), 1)
                lagging = length + new_count - 1 - SINK - slot
                turn = cycle_size * (jnp.maximum(lagging, 0) // cycle_size)
                ahead = jnp.where(lagging >= 0, SINK + slot + turn - length, 1 << 20)
                lag = moment - ahead
                seen = (lag >= 0) & (lag < WINDOW)
                bias[:, begin : begin + size] = jnp.where(seen, 0.0, NEG)
            result = jnp.zeros((own_rows, lanes), jnp.float32)
            for head in range(lanes // HD):
                mine = lane_head == head
                picked = jnp.where(mine, queries.astype(jnp.float32), 0.0).astype(jnp.bfloat16)
                sink_scores = (
                    lax.dot_general(
                        picked, sink_ref[0], contract, preferred_element_type=jnp.float32
                    )
                    + sink_bias
                )
                highest = jnp.max(sink_scores, axis=-1, keepdims=True)
                for begin, size in zip(starts, sizes):
                    part = lax.dot_general(
                        picked,
                        cycle_ref[0, begin : begin + size, :],
                        contract,
                        preferred_element_type=jnp.float32,
                    )
                    part = part + bias[:, begin : begin + size]
                    scores[:, begin : begin + size] = part
                    highest = jnp.maximum(highest, jnp.max(part, axis=-1, keepdims=True))
                weights = jnp.exp(sink_scores - highest)
                total = jnp.sum(weights, axis=-1, keepdims=True)
                summed = jnp.dot(
                    weights.astype(jnp.bfloat16), sink_ref[1], preferred_element_type=jnp.float32
                )
                for begin, size in zip(starts, sizes):
                    weights = jnp.exp(scores[:, begin : begin + size] - highest)
                    total += jnp.sum(weights, axis=-1, keepdims=True)
                    summed += jnp.dot(
                        weights.astype(jnp.bfloat16),
                        cycle_ref[1, begin : begin + size, :],
                        preferred_element_type=jnp.float32,
                    )
                result = jnp.where(mine, summed / total, result)
            out_ref[pl.ds(at, own_rows), :] = result.astype(jnp.bfloat16)
            return 0

        lax.fori_loop(0, new_count // own_rows, tile, 0)

    few = length + new_count - SINK <= SHORT_KEYS

    @pl.when(few)
    def _():
        run(SHORT_KEYS)

    @pl.when(jnp.logical_not(few))
    def _():
        run(cycle_size)


def mix_kernel(spots, count, parts, own_rows, rows, scalars, *refs):
    attended, pieces = refs[:parts], refs[parts : parts + count]
    kept_ref, sent_ref, held = refs[parts + count :]
    place(scalars, pieces, spots, held)
    wide = jnp.concatenate([ref[rows, :] for ref in attended], axis=1)
    mixed = lax.dot_general(
        wide, held[...], (((1,), (1,)), ((), ())), preferred_element_type=jnp.float32
    ).astype(jnp.bfloat16)
    split_rows(mixed, kept_ref, sent_ref, own_rows)


def units_kernel(spots, count, blocks, scalars, up_scale, gate_scale, *refs):
    pieces, row_refs = refs[:count], refs[count : count + blocks]
    out_ref, held = refs[count + blocks :]
    rows = jnp.concatenate([ref[...] for ref in row_refs], axis=0)
    for plane in range(2):
        place(scalars, pieces, spots, held.at[plane], (plane,))
    up = jnp.dot(rows, held[0], preferred_element_type=jnp.float32) * up_scale[...]
    gate = jnp.dot(rows, held[1], preferred_element_type=jnp.float32) * gate_scale[...]
    out_ref[...] = (up * (gate / (1.0 + jnp.exp(-gate)))).astype(jnp.bfloat16)


def lower_kernel(spots, counts, own_rows, rows, scalars, active_ref, *refs):
    kept_ref, sent_ref, held = refs[sum(counts) :]
    lane = 0
    for n, count in enumerate(counts):
        pieces = refs[sum(counts[:n]) : sum(counts[: n + 1])]
        place(scalars, pieces, spots[n], held, lane=lane)
        lane += pieces[0].shape[-1]
    lowered = lax.dot_general(
        active_ref[rows, :], held[...], (((1,), (1,)), ((), ())), preferred_element_type=jnp.float32
    ).astype(jnp.bfloat16)
    split_rows(lowered, kept_ref, sent_ref, own_rows)


def per_device(
    axes,
    hidden,
    lengths,
    sink_kv,
    kv_cycle,
    w_qkv,
    s_qk,
    w_out,
    alpha_attn,
    w_up,
    w_gate,
    s_up,
    s_gate,
    w_down,
    alpha_mlp,
):
    here = Layout(*axes)
    _, own_rows, model_width = hidden.shape
    nx, blocks = here.nx, axes[0]
    new_count = own_rows * blocks
    local_cols = s_qk.shape[0]
    cycle_size = kv_cycle.shape[2]
    units = s_up.shape[0]
    lanes = min(128, local_cols)
    parts = local_cols // lanes
    span = min(new_count + 16, cycle_size)
    chunk = cycle_size // 9

    row_blocks = []
    for d in range(nx):
        block = here.to_x(hidden[0], d) if d else hidden[0]
        row_blocks += [block, here.swap_core(block)]

    qkv_arrays, qkv_spots = pieces_of(here.gather(w_qkv.transpose(1, 0, 2)))
    out_arrays, out_spots = pieces_of(here.gather_y_first(w_out.T))
    gated_arrays, gated_spots = pieces_of(here.gather(jnp.stack([w_up, w_gate])))
    lower_t = w_down.T
    half = units // 2
    first_arrays, first_spots = pieces_of(here.gather_y_first(lower_t[:, :half]))
    second_arrays, second_spots = pieces_of(here.gather(lower_t[:, half:]))

    scalars = jnp.stack([lengths[0], here.x, here.c, jnp.int32(nx), *here.blocks()])
    staged = pl.pallas_call(
        stage_kernel,
        grid=(9,),
        out_shape=jax.ShapeDtypeStruct(kv_cycle.shape[1:], jnp.bfloat16),
        in_specs=[pl.BlockSpec((2, chunk, local_cols), lambda n: (0, n, 0))],
        out_specs=pl.BlockSpec((2, chunk, local_cols), lambda n: (0, n, 0)),
        compiler_params=PARAMS,
        name="stage",
    )(kv_cycle[0])
    queries, new_cycle = pl.pallas_call(
        functools.partial(qkv_kernel, qkv_spots, len(qkv_arrays), blocks, own_rows),
        out_shape=(
            jax.ShapeDtypeStruct((new_count, local_cols), jnp.bfloat16),
            jax.ShapeDtypeStruct(kv_cycle.shape[1:], jnp.bfloat16),
        ),
        in_specs=[SMEM, VMEM, ANY] + [VMEM] * (len(qkv_arrays) + blocks),
        out_specs=(VMEM, ANY),
        scratch_shapes=[
            pltpu.VMEM((2, span, local_cols), jnp.bfloat16),
            pltpu.VMEM((2, new_count, local_cols), jnp.bfloat16),
            pltpu.VMEM((3, model_width, local_cols), jnp.bfloat16),
            pltpu.SemaphoreType.DMA((2,)),
        ],
        input_output_aliases={2: 1},
        compiler_params=PARAMS,
        name="qkv",
    )(scalars, s_qk[None], staged, *qkv_arrays, *row_blocks)

    sinks = jnp.pad(sink_kv[0], ((0, 0), (0, 128 - SINK), (0, 0)))
    attended = [
        pl.pallas_call(
            functools.partial(attention_kernel, own_rows),
            grid=(1,),
            out_shape=jax.ShapeDtypeStruct((new_count, lanes), jnp.bfloat16),
            in_specs=[
                SMEM,
                pl.BlockSpec((new_count, lanes), lambda _, part=part: (0, part)),
                pl.BlockSpec((2, cycle_size, lanes), lambda _, part=part: (0, 0, part)),
                pl.BlockSpec((2, 128, lanes), lambda _, part=part: (0, 0, part)),
            ],
            out_specs=pl.BlockSpec((new_count, lanes), lambda _: (0, 0)),
            scratch_shapes=[
                pltpu.VMEM((own_rows, cycle_size), jnp.float32),
                pltpu.VMEM((own_rows, cycle_size), jnp.float32),
            ],
            compiler_params=PARAMS,
        )(scalars, queries, new_cycle, sinks)
        for part in range(parts)
    ]

    groups = {"a": slice(2 * own_rows, new_count), "b": slice(0, 2 * own_rows)}

    def halves(rows):
        size = (rows.stop - rows.start) // 2
        return (jax.ShapeDtypeStruct((size, model_width), jnp.bfloat16),) * 2

    def mix(group):
        rows = groups[group]
        return pl.pallas_call(
            functools.partial(mix_kernel, out_spots, len(out_arrays), parts, own_rows, rows),
            out_shape=halves(rows),
            in_specs=[SMEM] + [VMEM] * (parts + len(out_arrays)),
            out_specs=(VMEM, VMEM),
            scratch_shapes=[pltpu.VMEM((model_width, local_cols), jnp.bfloat16)],
            compiler_params=PARAMS,
        )(scalars, *attended, *out_arrays)

    far = here.core_sum(mix("a"))
    near = here.core_sum(mix("b"))
    sums = [part.astype(jnp.bfloat16) for part in [near, *jnp.split(far, nx - 1)]]
    totals = [part.astype(jnp.float32) for part in sums]
    for step in range(1, nx):
        for d in reversed(range(nx)):
            moved = here.to_x(sums[d], step)
            totals[(d + step) % nx] += moved.astype(jnp.float32)
    after = []
    after_blocks = []
    for d in range(nx):
        residual = row_blocks[2 * d].astype(jnp.float32)
        stepped = residual + alpha_attn * (rms_unit(totals[d]) - residual)
        after.append(rms_unit(stepped).astype(jnp.bfloat16))
        after_blocks += [after[d], here.swap_core(after[d])]

    tile = 256 if units % 256 == 0 else 128
    piece_rows = gated_arrays[0].shape[1]
    active = pl.pallas_call(
        functools.partial(units_kernel, gated_spots, len(gated_arrays), blocks),
        grid=(units // tile,),
        out_shape=jax.ShapeDtypeStruct((new_count, units), jnp.bfloat16),
        in_specs=[SMEM]
        + [pl.BlockSpec((1, tile), lambda n: (0, n))] * 2
        + [pl.BlockSpec((2, piece_rows, tile), lambda n: (0, 0, n))] * len(gated_arrays)
        + [pl.BlockSpec((own_rows, model_width), lambda n: (0, 0))] * blocks,
        out_specs=pl.BlockSpec((new_count, tile), lambda n: (0, n)),
        scratch_shapes=[pltpu.VMEM((2, model_width, tile), jnp.bfloat16)],
        compiler_params=PARAMS,
        name="units",
    )(scalars, s_up[None], s_gate[None], *gated_arrays, *after_blocks)

    down_arrays = [*first_arrays, *second_arrays]

    def lower(group):
        rows = groups[group]
        counts = (len(first_arrays), len(second_arrays))
        return pl.pallas_call(
            functools.partial(lower_kernel, (first_spots, second_spots), counts, own_rows, rows),
            out_shape=halves(rows),
            in_specs=[SMEM] + [VMEM] * (1 + len(down_arrays)),
            out_specs=(VMEM, VMEM),
            scratch_shapes=[pltpu.VMEM((model_width, units), jnp.bfloat16)],
            compiler_params=PARAMS,
        )(scalars, active, *down_arrays)

    far = jnp.split(here.core_sum(lower("a")), nx - 1)
    lowered = here.core_sum(lower("b"))
    for d in range(1, nx):
        moved = here.to_x(far[d - 1].astype(jnp.bfloat16), -d)
        lowered += moved.astype(jnp.float32)
    own_wide = after[0].astype(jnp.float32)
    result = rms_unit(own_wide + alpha_mlp * (rms_unit(lowered) - own_wide)).astype(jnp.bfloat16)
    return (result[None], new_cycle[None])


def solution(mesh):
    axes = (mesh.shape["gx"], mesh.shape["gy"])

    def body(*args):
        return per_device(axes, *args)

    return jax.shard_map(
        body,
        mesh=mesh,
        in_specs=(
            P("gy", "gx", None),
            P("gy"),
            P("gy", None, None, "gx"),
            P("gy", None, None, "gx"),
            P("gy", None, "gx"),
            P("gx"),
            P("gx", "gy"),
            P(),
            P("gy", "gx"),
            P("gy", "gx"),
            P("gx"),
            P("gx"),
            P("gx", "gy"),
            P(),
        ),
        out_specs=(P("gy", "gx", None), P("gy", None, None, "gx")),
        check_vma=False,
    )
```

profile of v0, /device:TPU:0, one launch (start us, length us, event | category | flops | bytes accessed | tf_op | source)
XLA Modules:
  0.0 252.4 jit_solution(10057503077699259915)
XLA Ops:
  0.6 5.1 %collective-permute-start.1 = (bf16[3,160,256]{2,1,0:T(8,128)(2,1)}, bf16[3,160,256]{2,1,0:T(8,128)(2,1)S(1)}, u32[]{:S(2)}, u32[]{:S(2)}) collective-permute-start(bf16[3,160,256]{2,1,0:T(8,128)(2,1)} %bitcast.38), channel_id=1, source_target_pairs={{0,6},{1,7},{2,0},{3,1},{4,2},{5,3},{6,4},{7,5},{8,14},{9,15},{10,... | collective-permute-start | bytes 737288 | tf_op jit(solution)/shard_map/ppermute | solution.py:45
  5.8 5.5 %collective-permute-done.1.rest_2_ = bf16[3,160,256]{2,1,0:T(8,128)(2,1)S(1)} collective-permute-done((bf16[3,160,256]{2,1,0:T(8,128)(2,1)}, bf16[3,160,256]{2,1,0:T(8,128)(2,1)S(1)}, u32[]{:S(2)}, u32[]{:S(2)}) %collective-permute-start.1) | collective-permute-done | bytes 245792 | tf_op jit(solution)/shard_map/ppermute | solution.py:45
  11.3 4.2 %collective-permute-start.3 = (bf16[3,160,256]{2,1,0:T(8,128)(2,1)S(1)}, bf16[3,160,256]{2,1,0:T(8,128)(2,1)S(1)}, u32[]{:S(2)}, u32[]{:S(2)}) collective-permute-start(bf16[3,160,256]{2,1,0:T(8,128)(2,1)S(1)} %collective-permute-done.1.rest_2_), channel_id=1, source_target_pairs={{0,6},{1,7},{2,0},{3,1},{4,2},{5,3},{6,4},{7,5},{8,14},{9,15},{10,... | collective-permute-start | bytes 737288 | tf_op jit(solution)/shard_map/ppermute | solution.py:45
  19.8 4.3 %collective-permute-start.5 = (bf16[3,160,256]{2,1,0:T(8,128)(2,1)S(1)}, bf16[3,160,256]{2,1,0:T(8,128)(2,1)S(1)}, u32[]{:S(2)}, u32[]{:S(2)}) collective-permute-start(bf16[3,160,256]{2,1,0:T(8,128)(2,1)S(1)} %collective-permute-done.3.rest_4_), channel_id=1, source_target_pairs={{0,6},{1,7},{2,0},{3,1},{4,2},{5,3},{6,4},{7,5},{8,14},{9,15},{10,... | collective-permute-start | bytes 737288 | tf_op jit(solution)/shard_map/ppermute | solution.py:45
  25.2 5.9 %collective-permute-done.11.refs_3_ = bf16[2,160,256]{2,1,0:T(8,128)(2,1)S(1)} collective-permute-done((bf16[2,160,256]{2,1,0:T(8,128)(2,1)S(1)}, bf16[2,160,256]{2,1,0:T(8,128)(2,1)S(1)}, u32[]{:S(2)}, u32[]{:S(2)}) %collective-permute-start.11) | collective-permute-done | bytes 163872 | tf_op jit(solution)/shard_map/ppermute | solution.py:45
  31.1 4.3 %collective-permute-start.12 = (bf16[2,160,256]{2,1,0:T(8,128)(2,1)S(1)}, bf16[2,160,256]{2,1,0:T(8,128)(2,1)S(1)}, u32[]{:S(2)}, u32[]{:S(2)}) collective-permute-start(bf16[2,160,256]{2,1,0:T(8,128)(2,1)S(1)} %collective-permute-done.11.refs_3_), channel_id=1, source_target_pairs={{0,6},{1,7},{2,0},{3,1},{4,2},{5,3},{6,4},{7,5},{8,14},{9,15},{10,... | collective-permute-start | bytes 491528 | tf_op jit(solution)/shard_map/ppermute | solution.py:45
  39.0 3.5 %collective-permute-start.13 = (bf16[2,160,256]{2,1,0:T(8,128)(2,1)S(1)}, bf16[2,160,256]{2,1,0:T(8,128)(2,1)S(1)}, u32[]{:S(2)}, u32[]{:S(2)}) collective-permute-start(bf16[2,160,256]{2,1,0:T(8,128)(2,1)S(1)} %collective-permute-done.12.refs_4_), channel_id=1, source_target_pairs={{0,6},{1,7},{2,0},{3,1},{4,2},{5,3},{6,4},{7,5},{8,14},{9,15},{10,... | collective-permute-start | bytes 491528 | tf_op jit(solution)/shard_map/ppermute | solution.py:45
  43.2 7.3 %stage.1.cycle_in = bf16[2,4608,256]{2,1,0:T(8,128)(2,1)} custom-call(bf16[2,4608,256]{2,1,0:T(8,128)(2,1)} %bitcast.31), custom_call_target="tpu_custom_call" | custom-call | tf_op jit(solution)/shard_map/stage/pallas_call | solution.py:355
  52.9 6.2 %qkv.1 = (bf16[512,256]{1,0:T(8,128)(2,1)}, bf16[2,4608,256]{2,1,0:T(8,128)(2,1)}) custom-call(s32[12]{0:T(128)} %stack.70.scalars, f32[1,256]{1,0:T(1,128)} %bitcast.46, bf16[2,4608,256]{2,1,0:T(8,128)(2,1)} %stage.1.cycle_in, bf16[3,160,256]{2,1,0:T(8,128)(2,1)} %bitcast.40, bf16[3,160,256]{2,1,0:T(8,128)(2,1)} %copy-done.38, ...), custom_call_target="tpu_custom_call", output_to_operand_aliasing={{1}: (2, {})} | custom-call | tf_op jit(solution)/shard_map/qkv/pallas_call | solution.py:364
  59.1 5.8 %shard_map.150.refs_1_ = bf16[512,128]{1,0:T(8,128)(2,1)} custom-call(s32[12]{0:T(128)} %stack.70.scalars, bf16[512,256]{1,0:T(8,128)(2,1)} %get-tuple-element.12.query_ref, bf16[2,4608,256]{2,1,0:T(8,128)(2,1)} %get-tuple-element.13.cycle_ref, bf16[2,128,256]{2,1,0:T(8,128)(2,1)} %pad.4.sink_ref), custom_call_target="tpu_custom_call" | custom-call | tf_op jit(solution)/shard_map/pallas_call | solution.py:385
  64.9 5.8 %shard_map.149.refs_0_ = bf16[512,128]{1,0:T(8,128)(2,1)} custom-call(s32[12]{0:T(128)} %stack.70.scalars, bf16[512,256]{1,0:T(8,128)(2,1)} %get-tuple-element.12.query_ref, bf16[2,4608,256]{2,1,0:T(8,128)(2,1)} %get-tuple-element.13.cycle_ref, bf16[2,128,256]{2,1,0:T(8,128)(2,1)} %pad.4.sink_ref), custom_call_target="tpu_custom_call" | custom-call | tf_op jit(solution)/shard_map/pallas_call | solution.py:385
  71.4 2.5 shard_map.152
  74.0 13.4 %collective-permute-start.18 = (bf16[2,160,1280]{2,1,0:T(8,128)(2,1)S(1)}, bf16[2,160,1280]{2,1,0:T(8,128)(2,1)S(1)}, u32[]{:S(2)}, u32[]{:S(2)}) collective-permute-start(bf16[2,160,1280]{2,1,0:T(8,128)(2,1)S(1)} %pad_maximum_fusion.refs_0_), channel_id=1, source_target_pairs={{0,6},{1,7},{2,0},{3,1},{4,2},{5,3},{6,4},{7,5},{8,14},{9,15},{10,... | collective-permute-start | bytes 2457608 | tf_op jit(solution)/shard_map/ppermute | solution.py:45
  87.5 2.5 %shard_map.151 = (bf16[128,1280]{1,0:T(8,128)(2,1)}, bf16[128,1280]{1,0:T(8,128)(2,1)}) custom-call(s32[12]{0:T(128)} %stack.70.scalars, bf16[512,128]{1,0:T(8,128)(2,1)} %shard_map.149.refs_0_, bf16[512,128]{1,0:T(8,128)(2,1)} %shard_map.150.refs_1_, bf16[2,160,256]{2,1,0:T(8,128)(2,1)} %copy-done.11, bf16[2,160,256]{2,1,0:T(8,128)(2,1)} %copy-done.27, ...), custom_call_target="tpu_custom_call" | custom-call | tf_op jit(solution)/shard_map/pallas_call | solution.py:413
  92.9 12.6 %collective-permute-done.18.refs_2_ = bf16[2,160,1280]{2,1,0:T(8,128)(2,1)S(1)} collective-permute-done((bf16[2,160,1280]{2,1,0:T(8,128)(2,1)S(1)}, bf16[2,160,1280]{2,1,0:T(8,128)(2,1)S(1)}, u32[]{:S(2)}, u32[]{:S(2)}) %collective-permute-start.18) | collective-permute-done | bytes 819232 | tf_op jit(solution)/shard_map/ppermute | solution.py:45
  105.5 4.3 %collective-permute-start.20 = (bf16[2,160,1280]{2,1,0:T(8,128)(2,1)S(1)}, bf16[2,160,1280]{2,1,0:T(8,128)(2,1)S(1)}, u32[]{:S(2)}, u32[]{:S(2)}) collective-permute-start(bf16[2,160,1280]{2,1,0:T(8,128)(2,1)S(1)} %collective-permute-done.18.refs_2_), channel_id=1, source_target_pairs={{0,6},{1,7},{2,0},{3,1},{4,2},{5,3},{6,4},{7,5},{8,14},{9,15},{10,... | collective-permute-start | bytes 2457608 | tf_op jit(solution)/shard_map/ppermute | solution.py:45
  110.0 22.9 %collective-permute-done.32.refs_6_ = bf16[160,640]{1,0:T(8,128)(2,1)S(1)} collective-permute-done((bf16[160,640]{1,0:T(8,128)(2,1)S(1)}, bf16[160,640]{1,0:T(8,128)(2,1)S(1)}, u32[]{:S(2)}, u32[]{:S(2)}) %collective-permute-start.32) | collective-permute-done | bytes 204832 | tf_op jit(solution)/shard_map/ppermute | solution.py:45
  132.8 4.3 %collective-permute-start.34 = (bf16[160,640]{1,0:T(8,128)(2,1)S(1)}, bf16[160,640]{1,0:T(8,128)(2,1)S(1)}, u32[]{:S(2)}, u32[]{:S(2)}) collective-permute-start(bf16[160,640]{1,0:T(8,128)(2,1)S(1)} %collective-permute-done.32.refs_6_), channel_id=1, source_target_pairs={{0,6},{1,7},{2,0},{3,1},{4,2},{5,3},{6,4},{7,5},{8,14},{9,15},{10,... | collective-permute-start | bytes 614408 | tf_op jit(solution)/shard_map/ppermute | solution.py:45
  139.9 4.8 %collective-permute-done.34.refs_8_ = bf16[160,640]{1,0:T(8,128)(2,1)S(1)} collective-permute-done((bf16[160,640]{1,0:T(8,128)(2,1)S(1)}, bf16[160,640]{1,0:T(8,128)(2,1)S(1)}, u32[]{:S(2)}, u32[]{:S(2)}) %collective-permute-start.34) | collective-permute-done | bytes 204832 | tf_op jit(solution)/shard_map/ppermute | solution.py:45
  144.7 4.3 %collective-permute-start.36 = (bf16[160,640]{1,0:T(8,128)(2,1)S(1)}, bf16[160,640]{1,0:T(8,128)(2,1)S(1)}, u32[]{:S(2)}, u32[]{:S(2)}) collective-permute-start(bf16[160,640]{1,0:T(8,128)(2,1)S(1)} %collective-permute-done.34.refs_8_), channel_id=1, source_target_pairs={{0,6},{1,7},{2,0},{3,1},{4,2},{5,3},{6,4},{7,5},{8,14},{9,15},{10,... | collective-permute-start | bytes 614408 | tf_op jit(solution)/shard_map/ppermute | solution.py:45
  150.0 4.4 %collective-permute-done.36.refs_10_ = bf16[160,640]{1,0:T(8,128)(2,1)S(1)} collective-permute-done((bf16[160,640]{1,0:T(8,128)(2,1)S(1)}, bf16[160,640]{1,0:T(8,128)(2,1)S(1)}, u32[]{:S(2)}, u32[]{:S(2)}) %collective-permute-start.36) | collective-permute-done | bytes 204832 | tf_op jit(solution)/shard_map/ppermute | solution.py:45
  154.4 24.1 %collective-permute-done.22.refs_6_ = bf16[2,160,1280]{2,1,0:T(8,128)(2,1)S(1)} collective-permute-done((bf16[2,160,1280]{2,1,0:T(8,128)(2,1)S(1)}, bf16[2,160,1280]{2,1,0:T(8,128)(2,1)S(1)}, u32[]{:S(2)}, u32[]{:S(2)}) %collective-permute-start.22) | collective-permute-done | bytes 819232 | tf_op jit(solution)/shard_map/ppermute | solution.py:45
  179.7 4.3 %collective-permute-start.30 = (bf16[2,160,640]{2,1,0:T(8,128)(2,1)S(1)}, bf16[2,160,640]{2,1,0:T(8,128)(2,1)S(1)}, u32[]{:S(2)}, u32[]{:S(2)}) collective-permute-start(bf16[2,160,640]{2,1,0:T(8,128)(2,1)S(1)} %collective-permute-done.29.refs_2_), channel_id=1, source_target_pairs={{0,6},{1,7},{2,0},{3,1},{4,2},{5,3},{6,4},{7,5},{8,14},{9,15},{10,... | collective-permute-start | bytes 1228808 | tf_op jit(solution)/shard_map/ppermute | solution.py:45
  184.0 2.0 collective-permute-start.31
  186.1 10.0 %collective-permute-done.21.refs_5_ = bf16[2,160,1280]{2,1,0:T(8,128)(2,1)S(1)} collective-permute-done((bf16[2,160,1280]{2,1,0:T(8,128)(2,1)S(1)}, bf16[2,160,1280]{2,1,0:T(8,128)(2,1)S(1)}, u32[]{:S(2)}, u32[]{:S(2)}) %collective-permute-start.21) | collective-permute-done | bytes 819232 | tf_op jit(solution)/shard_map/ppermute | solution.py:53
  196.1 17.5 %collective-permute-done.23.refs_7_ = bf16[2,160,1280]{2,1,0:T(8,128)(2,1)S(1)} collective-permute-done((bf16[2,160,1280]{2,1,0:T(8,128)(2,1)S(1)}, bf16[2,160,1280]{2,1,0:T(8,128)(2,1)S(1)}, u32[]{:S(2)}, u32[]{:S(2)}) %collective-permute-start.23) | collective-permute-done | bytes 819232 | tf_op jit(solution)/shard_map/ppermute | solution.py:53
  215.8 8.7 %units.1.active_ref = bf16[512,1280]{1,0:T(8,128)(2,1)} custom-call(s32[12]{0:T(128)} %stack.70.scalars, f32[1,1280]{1,0:T(1,128)} %broadcast_in_dim.11.up_scale, f32[1,1280]{1,0:T(1,128)} %broadcast_in_dim.12.gate_scale, bf16[2,160,1280]{2,1,0:T(8,128)(2,1)} %copy-done.3, bf16[2,160,1280]{2,1,0:T(8,128)(2,1)} %copy-done.15, ...), custom_call_target="tpu_custom_call" | custom-call | tf_op jit(solution)/shard_map/units/pallas_call | solution.py:440
  224.9 2.2 collective-permute-done.37.refs_11_
  228.6 4.4 %shard_map.154 = (bf16[128,1280]{1,0:T(8,128)(2,1)}, bf16[128,1280]{1,0:T(8,128)(2,1)}) custom-call(s32[12]{0:T(128)} %stack.70.scalars, bf16[512,1280]{1,0:T(8,128)(2,1)} %units.1.active_ref, bf16[2,160,640]{2,1,0:T(8,128)(2,1)} %copy-done.2, bf16[2,160,640]{2,1,0:T(8,128)(2,1)} %copy-done.8, bf16[2,160,640]{2,1,0:T(8,128)(2,1)} %copy-done.9, ...), custom_call_target="tpu_custom_call" | custom-call | tf_op jit(solution)/shard_map/pallas_call | solution.py:459
  233.0 4.4 %shard_map.153 = (bf16[128,1280]{1,0:T(8,128)(2,1)}, bf16[128,1280]{1,0:T(8,128)(2,1)}) custom-call(s32[12]{0:T(128)} %stack.70.scalars, bf16[512,1280]{1,0:T(8,128)(2,1)} %units.1.active_ref, bf16[2,160,640]{2,1,0:T(8,128)(2,1)} %copy-done.2, bf16[2,160,640]{2,1,0:T(8,128)(2,1)} %copy-done.8, bf16[2,160,640]{2,1,0:T(8,128)(2,1)} %copy-done.9, ...), custom_call_target="tpu_custom_call" | custom-call | tf_op jit(solution)/shard_map/pallas_call | solution.py:459
  239.4 8.3 %collective-permute-done.40 = bf16[128,1280]{1,0:T(8,128)(2,1)S(1)} collective-permute-done((bf16[128,1280]{1,0:T(8,128)(2,1)S(1)}, bf16[128,1280]{1,0:T(8,128)(2,1)S(1)}, u32[]{:S(2)}, u32[]{:S(2)}) %collective-permute-start.40) | collective-permute-done | bytes 327712 | tf_op jit(solution)/shard_map/ppermute | solution.py:59
  250.3 2.0 fusion.3
  (177 shorter events, 28.5 us)
Async XLA Ops:
  0.6 10.7 %collective-permute-start.1 = (bf16[3,160,256]{2,1,0:T(8,128)(2,1)}, bf16[3,160,256]{2,1,0:T(8,128)(2,1)S(1)}, u32[]{:S(2)}, u32[]{:S(2)}) collective-permute-start(bf16[3,160,256]{2,1,0:T(8,128)(2,1)} %bitcast.38), channel_id=1, source_target_pairs={{0,6},{1,7},{2,0},{3,1},{4,2},{5,3},{6,4},{7,5},{8,14},{9,15},{10,... | collective-permute-start | bytes 737288 | tf_op jit(solution)/shard_map/ppermute | solution.py:45
  18.5 18.5 %collective-permute-start.7 = (bf16[128,1280]{1,0:T(8,128)(2,1)}, bf16[128,1280]{1,0:T(8,128)(2,1)S(1)}, u32[]{:S(2)}, u32[]{:S(2)}) collective-permute-start(bf16[128,1280]{1,0:T(8,128)(2,1)} %bitcast.33), channel_id=1, source_target_pairs={{0,8},{8,0},{16,24},{24,16},{1,9},{9,1},{17,25},{25,17},{2,10},{10... | collective-permute-start | bytes 983048 | tf_op jit(solution)/shard_map/ppermute | solution.py:63
  18.5 16.9 %collective-permute-start = (bf16[3,160,256]{2,1,0:T(8,128)(2,1)}, bf16[3,160,256]{2,1,0:T(8,128)(2,1)S(1)}, u32[]{:S(2)}, u32[]{:S(2)}) collective-permute-start(bf16[3,160,256]{2,1,0:T(8,128)(2,1)} %bitcast.39), channel_id=1, source_target_pairs={{0,1},{1,0},{2,3},{3,2},{4,5},{5,4},{6,7},{7,6},{8,9},{9,8},{10,11... | collective-permute-start | bytes 737288 | tf_op jit(solution)/shard_map/ppermute | solution.py:53
  19.8 17.6 %collective-permute-start.5 = (bf16[3,160,256]{2,1,0:T(8,128)(2,1)S(1)}, bf16[3,160,256]{2,1,0:T(8,128)(2,1)S(1)}, u32[]{:S(2)}, u32[]{:S(2)}) collective-permute-start(bf16[3,160,256]{2,1,0:T(8,128)(2,1)S(1)} %collective-permute-done.3.rest_4_), channel_id=1, source_target_pairs={{0,6},{1,7},{2,0},{3,1},{4,2},{5,3},{6,4},{7,5},{8,14},{9,15},{10,... | collective-permute-start | bytes 737288 | tf_op jit(solution)/shard_map/ppermute | solution.py:45
  25.2 26.7 %collective-permute-start.9 = (bf16[128,1280]{1,0:T(8,128)(2,1)S(1)}, bf16[128,1280]{1,0:T(8,128)(2,1)S(1)}, u32[]{:S(2)}, u32[]{:S(2)}) collective-permute-start(bf16[128,1280]{1,0:T(8,128)(2,1)S(1)} %collective-permute-done.8.rest_10_), channel_id=1, source_target_pairs={{0,8},{8,0},{16,24},{24,16},{1,9},{9,1},{17,25},{25,17},{2,10},{10... | collective-permute-start | bytes 983048 | tf_op jit(solution)/shard_map/ppermute | solution.py:63
  35.4 16.5 %collective-permute-start.2 = (bf16[3,160,256]{2,1,0:T(8,128)(2,1)S(1)}, bf16[3,160,256]{2,1,0:T(8,128)(2,1)S(1)}, u32[]{:S(2)}, u32[]{:S(2)}) collective-permute-start(bf16[3,160,256]{2,1,0:T(8,128)(2,1)S(1)} %collective-permute-done.1.rest_2_), channel_id=1, source_target_pairs={{0,1},{1,0},{2,3},{3,2},{4,5},{5,4},{6,7},{7,6},{8,9},{9,8},{10,11... | collective-permute-start | bytes 737288 | tf_op jit(solution)/shard_map/ppermute | solution.py:53
  36.9 15.0 %collective-permute-start.4 = (bf16[3,160,256]{2,1,0:T(8,128)(2,1)S(1)}, bf16[3,160,256]{2,1,0:T(8,128)(2,1)S(1)}, u32[]{:S(2)}, u32[]{:S(2)}) collective-permute-start(bf16[3,160,256]{2,1,0:T(8,128)(2,1)S(1)} %collective-permute-done.3.rest_4_), channel_id=1, source_target_pairs={{0,1},{1,0},{2,3},{3,2},{4,5},{5,4},{6,7},{7,6},{8,9},{9,8},{10,11... | collective-permute-start | bytes 737288 | tf_op jit(solution)/shard_map/ppermute | solution.py:53
  37.4 14.5 %collective-permute-start.6 = (bf16[3,160,256]{2,1,0:T(8,128)(2,1)S(1)}, bf16[3,160,256]{2,1,0:T(8,128)(2,1)S(1)}, u32[]{:S(2)}, u32[]{:S(2)}) collective-permute-start(bf16[3,160,256]{2,1,0:T(8,128)(2,1)S(1)} %collective-permute-done.5.rest_6_), channel_id=1, source_target_pairs={{0,1},{1,0},{2,3},{3,2},{4,5},{5,4},{6,7},{7,6},{8,9},{9,8},{10,11... | collective-permute-start | bytes 737288 | tf_op jit(solution)/shard_map/ppermute | solution.py:53
  39.0 31.7 %collective-permute-start.13 = (bf16[2,160,256]{2,1,0:T(8,128)(2,1)S(1)}, bf16[2,160,256]{2,1,0:T(8,128)(2,1)S(1)}, u32[]{:S(2)}, u32[]{:S(2)}) collective-permute-start(bf16[2,160,256]{2,1,0:T(8,128)(2,1)S(1)} %collective-permute-done.12.refs_4_), channel_id=1, source_target_pairs={{0,6},{1,7},{2,0},{3,1},{4,2},{5,3},{6,4},{7,5},{8,14},{9,15},{10,... | collective-permute-start | bytes 491528 | tf_op jit(solution)/shard_map/ppermute | solution.py:45
  73.9 16.4 %collective-permute-start.15 = (bf16[128,1280]{1,0:T(8,128)(2,1)}, bf16[128,1280]{1,0:T(8,128)(2,1)S(1)}, u32[]{:S(2)}, u32[]{:S(2)}) collective-permute-start(bf16[128,1280]{1,0:T(8,128)(2,1)} %get-tuple-element.17), channel_id=1, source_target_pairs={{0,8},{8,0},{16,24},{24,16},{1,9},{9,1},{17,25},{25,17},{2,10},{10... | collective-permute-start | bytes 983048 | tf_op jit(solution)/shard_map/ppermute | solution.py:63
  74.0 31.5 %collective-permute-start.18 = (bf16[2,160,1280]{2,1,0:T(8,128)(2,1)S(1)}, bf16[2,160,1280]{2,1,0:T(8,128)(2,1)S(1)}, u32[]{:S(2)}, u32[]{:S(2)}) collective-permute-start(bf16[2,160,1280]{2,1,0:T(8,128)(2,1)S(1)} %pad_maximum_fusion.refs_0_), channel_id=1, source_target_pairs={{0,6},{1,7},{2,0},{3,1},{4,2},{5,3},{6,4},{7,5},{8,14},{9,15},{10,... | collective-permute-start | bytes 2457608 | tf_op jit(solution)/shard_map/ppermute | solution.py:45
  87.5 22.4 %collective-permute-start.27 = (bf16[160,640]{1,0:T(8,128)(2,1)S(1)}, bf16[160,640]{1,0:T(8,128)(2,1)S(1)}, u32[]{:S(2)}, u32[]{:S(2)}) collective-permute-start(bf16[160,640]{1,0:T(8,128)(2,1)S(1)} %get-tuple-element.28), channel_id=1, source_target_pairs={{0,1},{1,0},{2,3},{3,2},{4,5},{5,4},{6,7},{7,6},{8,9},{9,8},{10,11... | collective-permute-start | bytes 614408 | tf_op jit(solution)/shard_map/ppermute | solution.py:53
  90.1 47.1 %collective-permute-start.14 = (bf16[128,1280]{1,0:T(8,128)(2,1)}, bf16[128,1280]{1,0:T(8,128)(2,1)S(1)}, u32[]{:S(2)}, u32[]{:S(2)}) collective-permute-start(bf16[128,1280]{1,0:T(8,128)(2,1)} %get-tuple-element.15), channel_id=1, source_target_pairs={{0,8},{8,0},{16,24},{24,16},{1,9},{9,1},{17,25},{25,17},{2,10},{10... | collective-permute-start | bytes 983048 | tf_op jit(solution)/shard_map/ppermute | solution.py:63
  91.3 45.8 %collective-permute-start.16 = (bf16[128,1280]{1,0:T(8,128)(2,1)S(1)}, bf16[128,1280]{1,0:T(8,128)(2,1)S(1)}, u32[]{:S(2)}, u32[]{:S(2)}) collective-permute-start(bf16[128,1280]{1,0:T(8,128)(2,1)S(1)} %add_convert_fusion.1), channel_id=1, source_target_pairs={{0,16},{8,24},{16,0},{24,8},{1,17},{9,25},{17,1},{25,9},{2,18},{10... | collective-permute-start | bytes 983048 | tf_op jit(solution)/shard_map/ppermute | solution.py:59
  105.5 43.5 %collective-permute-start.20 = (bf16[2,160,1280]{2,1,0:T(8,128)(2,1)S(1)}, bf16[2,160,1280]{2,1,0:T(8,128)(2,1)S(1)}, u32[]{:S(2)}, u32[]{:S(2)}) collective-permute-start(bf16[2,160,1280]{2,1,0:T(8,128)(2,1)S(1)} %collective-permute-done.18.refs_2_), channel_id=1, source_target_pairs={{0,6},{1,7},{2,0},{3,1},{4,2},{5,3},{6,4},{7,5},{8,14},{9,15},{10,... | collective-permute-start | bytes 2457608 | tf_op jit(solution)/shard_map/ppermute | solution.py:45
  109.8 23.0 %collective-permute-start.32 = (bf16[160,640]{1,0:T(8,128)(2,1)S(1)}, bf16[160,640]{1,0:T(8,128)(2,1)S(1)}, u32[]{:S(2)}, u32[]{:S(2)}) collective-permute-start(bf16[160,640]{1,0:T(8,128)(2,1)S(1)} %get-tuple-element.26.refs_4_), channel_id=1, source_target_pairs={{0,6},{1,7},{2,0},{3,1},{4,2},{5,3},{6,4},{7,5},{8,14},{9,15},{10,... | collective-permute-start | bytes 614408 | tf_op jit(solution)/shard_map/ppermute | solution.py:45
  109.9 39.1 %collective-permute-start.28 = (bf16[2,160,640]{2,1,0:T(8,128)(2,1)S(1)}, bf16[2,160,640]{2,1,0:T(8,128)(2,1)S(1)}, u32[]{:S(2)}, u32[]{:S(2)}) collective-permute-start(bf16[2,160,640]{2,1,0:T(8,128)(2,1)S(1)} %pad_maximum_fusion.1.refs_0_), channel_id=1, source_target_pairs={{0,6},{1,7},{2,0},{3,1},{4,2},{5,3},{6,4},{7,5},{8,14},{9,15},{10,... | collective-permute-start | bytes 1228808 | tf_op jit(solution)/shard_map/ppermute | solution.py:45
  132.8 11.8 %collective-permute-start.34 = (bf16[160,640]{1,0:T(8,128)(2,1)S(1)}, bf16[160,640]{1,0:T(8,128)(2,1)S(1)}, u32[]{:S(2)}, u32[]{:S(2)}) collective-permute-start(bf16[160,640]{1,0:T(8,128)(2,1)S(1)} %collective-permute-done.32.refs_6_), channel_id=1, source_target_pairs={{0,6},{1,7},{2,0},{3,1},{4,2},{5,3},{6,4},{7,5},{8,14},{9,15},{10,... | collective-permute-start | bytes 614408 | tf_op jit(solution)/shard_map/ppermute | solution.py:45
  138.3 10.8 %collective-permute-start.25 = (bf16[128,1280]{1,0:T(8,128)(2,1)S(1)}, bf16[128,1280]{1,0:T(8,128)(2,1)S(1)}, u32[]{:S(2)}, u32[]{:S(2)}) collective-permute-start(bf16[128,1280]{1,0:T(8,128)(2,1)S(1)} %get-tuple-element.25), channel_id=1, source_target_pairs={{0,16},{8,24},{16,0},{24,8},{1,17},{9,25},{17,1},{25,9},{2,18},{10... | collective-permute-start | bytes 983048 | tf_op jit(solution)/shard_map/ppermute | solution.py:59
  139.9 39.3 %collective-permute-start.17 = (bf16[2,160,1280]{2,1,0:T(8,128)(2,1)S(1)}, bf16[2,160,1280]{2,1,0:T(8,128)(2,1)S(1)}, u32[]{:S(2)}, u32[]{:S(2)}) collective-permute-start(bf16[2,160,1280]{2,1,0:T(8,128)(2,1)S(1)} %pad_maximum_fusion.refs_0_), channel_id=1, source_target_pairs={{0,1},{1,0},{2,3},{3,2},{4,5},{5,4},{6,7},{7,6},{8,9},{9,8},{10,11... | collective-permute-start | bytes 2457608 | tf_op jit(solution)/shard_map/ppermute | solution.py:53
  144.7 9.7 %collective-permute-start.36 = (bf16[160,640]{1,0:T(8,128)(2,1)S(1)}, bf16[160,640]{1,0:T(8,128)(2,1)S(1)}, u32[]{:S(2)}, u32[]{:S(2)}) collective-permute-start(bf16[160,640]{1,0:T(8,128)(2,1)S(1)} %collective-permute-done.34.refs_8_), channel_id=1, source_target_pairs={{0,6},{1,7},{2,0},{3,1},{4,2},{5,3},{6,4},{7,5},{8,14},{9,15},{10,... | collective-permute-start | bytes 614408 | tf_op jit(solution)/shard_map/ppermute | solution.py:45
  149.0 30.3 %collective-permute-start.29 = (bf16[2,160,640]{2,1,0:T(8,128)(2,1)S(1)}, bf16[2,160,640]{2,1,0:T(8,128)(2,1)S(1)}, u32[]{:S(2)}, u32[]{:S(2)}) collective-permute-start(bf16[2,160,640]{2,1,0:T(8,128)(2,1)S(1)} %collective-permute-done.28.refs_1_), channel_id=1, source_target_pairs={{0,6},{1,7},{2,0},{3,1},{4,2},{5,3},{6,4},{7,5},{8,14},{9,15},{10,... | collective-permute-start | bytes 1228808 | tf_op jit(solution)/shard_map/ppermute | solution.py:45
  149.0 30.7 %collective-permute-start.19 = (bf16[2,160,1280]{2,1,0:T(8,128)(2,1)S(1)}, bf16[2,160,1280]{2,1,0:T(8,128)(2,1)S(1)}, u32[]{:S(2)}, u32[]{:S(2)}) collective-permute-start(bf16[2,160,1280]{2,1,0:T(8,128)(2,1)S(1)} %collective-permute-done.18.refs_2_), channel_id=1, source_target_pairs={{0,1},{1,0},{2,3},{3,2},{4,5},{5,4},{6,7},{7,6},{8,9},{9,8},{10,11... | collective-permute-start | bytes 2457608 | tf_op jit(solution)/shard_map/ppermute | solution.py:53
  149.1 29.4 %collective-permute-start.22 = (bf16[2,160,1280]{2,1,0:T(8,128)(2,1)S(1)}, bf16[2,160,1280]{2,1,0:T(8,128)(2,1)S(1)}, u32[]{:S(2)}, u32[]{:S(2)}) collective-permute-start(bf16[2,160,1280]{2,1,0:T(8,128)(2,1)S(1)} %collective-permute-done.20.refs_4_), channel_id=1, source_target_pairs={{0,6},{1,7},{2,0},{3,1},{4,2},{5,3},{6,4},{7,5},{8,14},{9,15},{10,... | collective-permute-start | bytes 2457608 | tf_op jit(solution)/shard_map/ppermute | solution.py:45
  154.4 41.7 %collective-permute-start.21 = (bf16[2,160,1280]{2,1,0:T(8,128)(2,1)S(1)}, bf16[2,160,1280]{2,1,0:T(8,128)(2,1)S(1)}, u32[]{:S(2)}, u32[]{:S(2)}) collective-permute-start(bf16[2,160,1280]{2,1,0:T(8,128)(2,1)S(1)} %collective-permute-done.20.refs_4_), channel_id=1, source_target_pairs={{0,1},{1,0},{2,3},{3,2},{4,5},{5,4},{6,7},{7,6},{8,9},{9,8},{10,11... | collective-permute-start | bytes 2457608 | tf_op jit(solution)/shard_map/ppermute | solution.py:53
  178.6 35.1 %collective-permute-start.23 = (bf16[2,160,1280]{2,1,0:T(8,128)(2,1)S(1)}, bf16[2,160,1280]{2,1,0:T(8,128)(2,1)S(1)}, u32[]{:S(2)}, u32[]{:S(2)}) collective-permute-start(bf16[2,160,1280]{2,1,0:T(8,128)(2,1)S(1)} %collective-permute-done.22.refs_6_), channel_id=1, source_target_pairs={{0,1},{1,0},{2,3},{3,2},{4,5},{5,4},{6,7},{7,6},{8,9},{9,8},{10,11... | collective-permute-start | bytes 2457608 | tf_op jit(solution)/shard_map/ppermute | solution.py:53
  179.7 47.4 %collective-permute-start.30 = (bf16[2,160,640]{2,1,0:T(8,128)(2,1)S(1)}, bf16[2,160,640]{2,1,0:T(8,128)(2,1)S(1)}, u32[]{:S(2)}, u32[]{:S(2)}) collective-permute-start(bf16[2,160,640]{2,1,0:T(8,128)(2,1)S(1)} %collective-permute-done.29.refs_2_), channel_id=1, source_target_pairs={{0,6},{1,7},{2,0},{3,1},{4,2},{5,3},{6,4},{7,5},{8,14},{9,15},{10,... | collective-permute-start | bytes 1228808 | tf_op jit(solution)/shard_map/ppermute | solution.py:45
  184.0 40.6 %collective-permute-start.31 = (bf16[160,640]{1,0:T(8,128)(2,1)S(1)}, bf16[160,640]{1,0:T(8,128)(2,1)S(1)}, u32[]{:S(2)}, u32[]{:S(2)}) collective-permute-start(bf16[160,640]{1,0:T(8,128)(2,1)S(1)} %get-tuple-element.26.refs_4_), channel_id=1, source_target_pairs={{0,1},{1,0},{2,3},{3,2},{4,5},{5,4},{6,7},{7,6},{8,9},{9,8},{10,11... | collective-permute-start | bytes 614408 | tf_op jit(solution)/shard_map/ppermute | solution.py:53
  186.1 38.6 %collective-permute-start.33 = (bf16[160,640]{1,0:T(8,128)(2,1)S(1)}, bf16[160,640]{1,0:T(8,128)(2,1)S(1)}, u32[]{:S(2)}, u32[]{:S(2)}) collective-permute-start(bf16[160,640]{1,0:T(8,128)(2,1)S(1)} %collective-permute-done.32.refs_6_), channel_id=1, source_target_pairs={{0,1},{1,0},{2,3},{3,2},{4,5},{5,4},{6,7},{7,6},{8,9},{9,8},{10,11... | collective-permute-start | bytes 614408 | tf_op jit(solution)/shard_map/ppermute | solution.py:53
  196.1 28.8 %collective-permute-start.35 = (bf16[160,640]{1,0:T(8,128)(2,1)S(1)}, bf16[160,640]{1,0:T(8,128)(2,1)S(1)}, u32[]{:S(2)}, u32[]{:S(2)}) collective-permute-start(bf16[160,640]{1,0:T(8,128)(2,1)S(1)} %collective-permute-done.34.refs_8_), channel_id=1, source_target_pairs={{0,1},{1,0},{2,3},{3,2},{4,5},{5,4},{6,7},{7,6},{8,9},{9,8},{10,11... | collective-permute-start | bytes 614408 | tf_op jit(solution)/shard_map/ppermute | solution.py:53
  213.7 13.5 %collective-permute-start.37 = (bf16[160,640]{1,0:T(8,128)(2,1)S(1)}, bf16[160,640]{1,0:T(8,128)(2,1)S(1)}, u32[]{:S(2)}, u32[]{:S(2)}) collective-permute-start(bf16[160,640]{1,0:T(8,128)(2,1)S(1)} %collective-permute-done.36.refs_10_), channel_id=1, source_target_pairs={{0,1},{1,0},{2,3},{3,2},{4,5},{5,4},{6,7},{7,6},{8,9},{9,8},{10,11... | collective-permute-start | bytes 614408 | tf_op jit(solution)/shard_map/ppermute | solution.py:53
  238.0 9.7 %collective-permute-start.40 = (bf16[128,1280]{1,0:T(8,128)(2,1)S(1)}, bf16[128,1280]{1,0:T(8,128)(2,1)S(1)}, u32[]{:S(2)}, u32[]{:S(2)}) collective-permute-start(bf16[128,1280]{1,0:T(8,128)(2,1)S(1)} %add_convert_fusion), channel_id=1, source_target_pairs={{0,16},{8,24},{16,0},{24,8},{1,17},{9,25},{17,1},{25,9},{2,18},{10... | collective-permute-start | bytes 983048 | tf_op jit(solution)/shard_map/ppermute | solution.py:59
  (57 other events, 1970.0 us)
where the time goes:
time: 253 us; the launch traced here: 252 us
  waiting for transfers between devices  120 us (47%)
  starting transfers between devices  66.6 us (26%)
  Pallas kernels  47.7 us (19%)
  other arithmetic  9.26 us (4%)
  local copies, waits for them, and re-layouts  6.66 us (3%)
    ppermute x15, waiting for transfers between devices, from_z(): return lax.ppermute(value, 'gy', pairs)  81.1 us
    ppermute x15, starting transfers between devices, from_z(): return lax.ppermute(value, 'gy', pairs)  52.3 us
    ppermute x14, waiting for transfers between devices, from_y(): return lax.ppermute(value, 'gy', pairs)  30 us
    pallas_call x2, Pallas kernels, per_device(): pl.pallas_call(functools.partial(attention_kernel, own_rows), grid=(1,),...  11.6 us
    pallas_call x2, Pallas kernels, lower(): pl.pallas_call(functools.partial(lower_kernel, (first_spots, second_spots...  8.85 us
    pallas_call x1, Pallas kernels, per_device(): pl.pallas_call(functools.partial(units_kernel, gated_spots, len(gated_arr...  8.74 us
    ppermute x4, waiting for transfers between devices, to_x(): return lax.ppermute(value, 'gx', pairs)  8.41 us
    ppermute x14, starting transfers between devices, from_y(): return lax.ppermute(value, 'gy', pairs)  7.82 us
  transfers between devices with their start and end apart: 41, of which 15 were waited for; matrix products, arithmetic and copies ran while one was open for 3% of the time, Pallas kernels for 16%

commit v1 on v0

--- a/solution.py
+++ b/solution.py
@@ -19,11 +19,7 @@
 VMEM = pl.BlockSpec(memory_space=pltpu.VMEM)
 SMEM = pl.BlockSpec(memory_space=pltpu.SMEM)
 ANY = pl.BlockSpec(memory_space=pl.ANY)
-PARAMS = pltpu.CompilerParams(vmem_limit_bytes=56 << 20)
-
-
-def rms_unit(values):
-    return values * lax.rsqrt(jnp.mean(values * values, axis=-1, keepdims=True) + 1e-06)
+PARAMS = pltpu.CompilerParams(vmem_limit_bytes=67043328)
 
 
 class Layout:
@@ -130,8 +126,26 @@
         sent_ref[at, :] = value[(2 * d + 1) * own_rows : (2 * d + 2) * own_rows]
 
 
-def stage_kernel(source, target):
+def rms_unit(values):
+    mean = jnp.sum(values * values, axis=-1, keepdims=True) * (1.0 / values.shape[-1])
+    return values * lax.rsqrt(mean + 1e-06)
+
+
+def step_towards(base, change, alpha):
+    return rms_unit(base + alpha * (rms_unit(change) - base)).astype(jnp.bfloat16)
+
+
+def stage_kernel(source, *rest):
+    target = rest[-1]
     target[...] = source[...]
+
+
+def norm_kernel(base_ref, alpha_ref, *refs):
+    terms, out_ref = refs[:-1], refs[-1]
+    change = terms[0][...].astype(jnp.float32)
+    for term in terms[1:]:
+        change += term[...].astype(jnp.float32)
+    out_ref[...] = step_towards(base_ref[...].astype(jnp.float32), change, alpha_ref[...])
 
 
 def qkv_kernel(spots, count, blocks, own_rows, scalars, scale_ref, cycle_in, *rest):
@@ -352,15 +366,20 @@
     second_arrays, second_spots = pieces_of(here.gather(lower_t[:, half:]))
 
     scalars = jnp.stack([lengths[0], here.x, here.c, jnp.int32(nx), *here.blocks()])
+    sinks = jnp.pad(sink_kv[0], ((0, 0), (0, 128 - SINK), (0, 0)))
+    vectors = [s_qk[None], s_up[None], s_gate[None], alpha_attn[None], alpha_mlp[None]]
+    early = [scalars, sinks, *vectors]
+    scale_qk, scale_up, scale_gate, alpha_attn, alpha_mlp = vectors
     staged = pl.pallas_call(
         stage_kernel,
         grid=(9,),
         out_shape=jax.ShapeDtypeStruct(kv_cycle.shape[1:], jnp.bfloat16),
-        in_specs=[pl.BlockSpec((2, chunk, local_cols), lambda n: (0, n, 0))],
+        in_specs=[pl.BlockSpec((2, chunk, local_cols), lambda n: (0, n, 0))]
+        + [ANY] * len(early),
         out_specs=pl.BlockSpec((2, chunk, local_cols), lambda n: (0, n, 0)),
         compiler_params=PARAMS,
         name="stage",
-    )(kv_cycle[0])
+    )(kv_cycle[0], *early)
     queries, new_cycle = pl.pallas_call(
         functools.partial(qkv_kernel, qkv_spots, len(qkv_arrays), blocks, own_rows),
         out_shape=(
@@ -378,9 +397,8 @@
         input_output_aliases={2: 1},
         compiler_params=PARAMS,
         name="qkv",
-    )(scalars, s_qk[None], staged, *qkv_arrays, *row_blocks)
-
-    sinks = jnp.pad(sink_kv[0], ((0, 0), (0, 128 - SINK), (0, 0)))
+    )(scalars, scale_qk, staged, *qkv_arrays, *row_blocks)
+
     attended = [
         pl.pallas_call(
             functools.partial(attention_kernel, own_rows),
@@ -422,17 +440,25 @@
     far = here.core_sum(mix("a"))
     near = here.core_sum(mix("b"))
     sums = [part.astype(jnp.bfloat16) for part in [near, *jnp.split(far, nx - 1)]]
-    totals = [part.astype(jnp.float32) for part in sums]
+    totals = [[part] for part in sums]
     for step in range(1, nx):
         for d in reversed(range(nx)):
             moved = here.to_x(sums[d], step)
-            totals[(d + step) % nx] += moved.astype(jnp.float32)
+            totals[(d + step) % nx].append(moved)
+
+    def norm(base, alpha, terms):
+        return pl.pallas_call(
+            norm_kernel,
+            out_shape=jax.ShapeDtypeStruct(base.shape, jnp.bfloat16),
+            in_specs=[VMEM] * (2 + len(terms)),
+            out_specs=VMEM,
+            compiler_params=PARAMS,
+        )(base, alpha, *terms)
+
     after = []
     after_blocks = []
     for d in range(nx):
-        residual = row_blocks[2 * d].astype(jnp.float32)
-        stepped = residual + alpha_attn * (rms_unit(totals[d]) - residual)
-        after.append(rms_unit(stepped).astype(jnp.bfloat16))
+        after.append(norm(row_blocks[2 * d], alpha_attn, totals[d]))
         after_blocks += [after[d], here.swap_core(after[d])]
 
     tile = 256 if units % 256 == 0 else 128
@@ -449,7 +475,7 @@
         scratch_shapes=[pltpu.VMEM((2, model_width, tile), jnp.bfloat16)],
         compiler_params=PARAMS,
         name="units",
-    )(scalars, s_up[None], s_gate[None], *gated_arrays, *after_blocks)
+    )(scalars, scale_up, scale_gate, *gated_arrays, *after_blocks)
 
     down_arrays = [*first_arrays, *second_arrays]
 
@@ -465,13 +491,11 @@
             compiler_params=PARAMS,
         )(scalars, active, *down_arrays)
 
-    far = jnp.split(here.core_sum(lower("a")), nx - 1)
-    lowered = here.core_sum(lower("b"))
-    for d in range(1, nx):
-        moved = here.to_x(far[d - 1].astype(jnp.bfloat16), -d)
-        lowered += moved.astype(jnp.float32)
-    own_wide = after[0].astype(jnp.float32)
-    result = rms_unit(own_wide + alpha_mlp * (rms_unit(lowered) - own_wide)).astype(jnp.bfloat16)
+    far = jnp.split(here.core_sum(lower("a")).astype(jnp.bfloat16), nx - 1)
+    kept, sent = lower("b")
+    terms = [kept, here.swap_core(sent)]
+    terms += [here.to_x(far[d - 1], -d) for d in range(1, nx)]
+    result = norm(after[0], alpha_mlp, terms)
     return (result[None], new_cycle[None])
 
 

time: 253 us -> 253 us (level)
  waiting for transfers between devices: 120 us -> 112 us
  Pallas kernels: 47.7 us -> 54.5 us
  local copies, waits for them, and re-layouts: 6.66 us -> 12.9 us
  starting transfers between devices: 66.6 us -> 64 us
    ppermute x15, waiting for transfers between devices: 81.1 us -> 66.1 us  [from_z(): return lax.ppermute(value, 'gy', pairs)]
    pallas_call x0 -> x3, Pallas kernels: none -> 6.95 us  [norm(): pl.pallas_call(norm_kernel, out_shape=jax.ShapeDtypeStruct(base.shape, jn...]
    ppermute x14, waiting for transfers between devices: 30 us -> 35.2 us  [from_y(): return lax.ppermute(value, 'gy', pairs)]
    ppermute x15, starting transfers between devices: 52.3 us -> 47.1 us  [from_z(): return lax.ppermute(value, 'gy', pairs)]
    reduce_sum x5 -> x0, other arithmetic: 4.49 us -> none  [rms_unit(): jnp.mean(values * values, axis=-1, keepdims=True) + 1e-06]
    ppermute x14, starting transfers between devices: 7.82 us -> 11.3 us  [from_y(): return lax.ppermute(value, 'gy', pairs)]
    broadcast_in_dim x0 -> x2, local copies, waits for them, and re-layouts: none -> 2.59 us  [the longest x1 1.3 us: per_device(): alpha_attn[None]]
  transfers between devices with their start and end apart: 41 -> 41, of which waited for: 15 -> 13; matrix products, arithmetic and copies ran while one was open for 3% -> 6% of each run, Pallas kernels for 16% -> 19%
where the time goes in v1:
time: 253 us; the launch traced here: 252 us
  waiting for transfers between devices  112 us (44%)
  starting transfers between devices  64 us (25%)
  Pallas kernels  54.5 us (22%)
  local copies, waits for them, and re-layouts  12.9 us (5%)
  other arithmetic  7.27 us (3%)
    ppermute x15, waiting for transfers between devices, from_z(): return lax.ppermute(value, 'gy', pairs)  66.1 us
    ppermute x15, starting transfers between devices, from_z(): return lax.ppermute(value, 'gy', pairs)  47.1 us
    ppermute x14, waiting for transfers between devices, from_y(): return lax.ppermute(value, 'gy', pairs)  35.2 us
    pallas_call x2, Pallas kernels, per_device(): pl.pallas_call(functools.partial(attention_kernel, own_rows), grid=(1,),...  11.5 us
    ppermute x14, starting transfers between devices, from_y(): return lax.ppermute(value, 'gy', pairs)  11.3 us
    ppermute x4, waiting for transfers between devices, to_x(): return lax.ppermute(value, 'gx', pairs)  10.6 us
    pallas_call x2, Pallas kernels, lower(): pl.pallas_call(functools.partial(lower_kernel, (first_spots, second_spots...  8.82 us
    pallas_call x1, Pallas kernels, per_device(): pl.pallas_call(functools.partial(units_kernel, gated_spots, len(gated_arr...  8.75 us
  transfers between devices with their start and end apart: 41, of which 13 were waited for; matrix products, arithmetic and copies ran while one was open for 6% of the time, Pallas kernels for 19%

profile of v1, /device:TPU:0, one launch (start us, length us, event | category | flops | bytes accessed | tf_op | source)
XLA Modules:
  0.0 252.2 jit_solution(811473301862524776)
XLA Ops:
  2.7 5.1 %collective-permute-start.18 = (bf16[2,160,1280]{2,1,0:T(8,128)(2,1)S(1)}, bf16[2,160,1280]{2,1,0:T(8,128)(2,1)}, u32[]{:S(2)}, u32[]{:S(2)}) collective-permute-start(bf16[2,160,1280]{2,1,0:T(8,128)(2,1)S(1)} %pad_maximum_fusion.refs_0_), channel_id=1, source_target_pairs={{0,6},{1,7},{2,0},{3,1},{4,2},{5,3},{6,4},{7,5},{8,14},{9,15},{10,... | collective-permute-start | bytes 2457608 | tf_op jit(solution)/shard_map/ppermute | solution.py:41
  11.8 5.6 %collective-permute-done.10 = bf16[160,256]{1,0:T(8,128)(2,1)S(1)} collective-permute-done((bf16[160,256]{1,0:T(8,128)(2,1)}, bf16[160,256]{1,0:T(8,128)(2,1)S(1)}, u32[]{:S(2)}, u32[]{:S(2)}) %collective-permute-start.10) | collective-permute-done | bytes 81952 | tf_op jit(solution)/shard_map/ppermute | solution.py:49
  17.4 13.3 %collective-permute-done.1.rest_2_ = bf16[3,160,256]{2,1,0:T(8,128)(2,1)S(1)} collective-permute-done((bf16[3,160,256]{2,1,0:T(8,128)(2,1)}, bf16[3,160,256]{2,1,0:T(8,128)(2,1)S(1)}, u32[]{:S(2)}, u32[]{:S(2)}) %collective-permute-start.1) | collective-permute-done | bytes 245792 | tf_op jit(solution)/shard_map/ppermute | solution.py:41
  30.7 4.2 %collective-permute-start.3 = (bf16[3,160,256]{2,1,0:T(8,128)(2,1)S(1)}, bf16[3,160,256]{2,1,0:T(8,128)(2,1)}, u32[]{:S(2)}, u32[]{:S(2)}) collective-permute-start(bf16[3,160,256]{2,1,0:T(8,128)(2,1)S(1)} %collective-permute-done.1.rest_2_), channel_id=1, source_target_pairs={{0,6},{1,7},{2,0},{3,1},{4,2},{5,3},{6,4},{7,5},{8,14},{9,15},{10,... | collective-permute-start | bytes 737288 | tf_op jit(solution)/shard_map/ppermute | solution.py:41
  35.9 6.8 %collective-permute-done.11.refs_3_ = bf16[2,160,256]{2,1,0:T(8,128)(2,1)S(1)} collective-permute-done((bf16[2,160,256]{2,1,0:T(8,128)(2,1)S(1)}, bf16[2,160,256]{2,1,0:T(8,128)(2,1)S(1)}, u32[]{:S(2)}, u32[]{:S(2)}) %collective-permute-start.11) | collective-permute-done | bytes 163872 | tf_op jit(solution)/shard_map/ppermute | solution.py:41
  44.3 4.3 %collective-permute-start.5 = (bf16[3,160,256]{2,1,0:T(8,128)(2,1)}, bf16[3,160,256]{2,1,0:T(8,128)(2,1)}, u32[]{:S(2)}, u32[]{:S(2)}) collective-permute-start(bf16[3,160,256]{2,1,0:T(8,128)(2,1)} %collective-permute-done.3.rest_4_), channel_id=1, source_target_pairs={{0,6},{1,7},{2,0},{3,1},{4,2},{5,3},{6,4},{7,5},{8,14},{9,15},{10,... | collective-permute-start | bytes 737288 | tf_op jit(solution)/shard_map/ppermute | solution.py:41
  49.4 23.8 %collective-permute-done.12.refs_4_ = bf16[2,160,256]{2,1,0:T(8,128)(2,1)} collective-permute-done((bf16[2,160,256]{2,1,0:T(8,128)(2,1)S(1)}, bf16[2,160,256]{2,1,0:T(8,128)(2,1)}, u32[]{:S(2)}, u32[]{:S(2)}) %collective-permute-start.12) | collective-permute-done | bytes 163872 | tf_op jit(solution)/shard_map/ppermute | solution.py:41
  73.1 4.4 %collective-permute-start.13 = (bf16[2,160,256]{2,1,0:T(8,128)(2,1)}, bf16[2,160,256]{2,1,0:T(8,128)(2,1)}, u32[]{:S(2)}, u32[]{:S(2)}) collective-permute-start(bf16[2,160,256]{2,1,0:T(8,128)(2,1)} %collective-permute-done.12.refs_4_), channel_id=1, source_target_pairs={{0,6},{1,7},{2,0},{3,1},{4,2},{5,3},{6,4},{7,5},{8,14},{9,15},{10,... | collective-permute-start | bytes 491528 | tf_op jit(solution)/shard_map/ppermute | solution.py:41
  90.1 7.3 %stage.1.cycle_in = bf16[2,4608,256]{2,1,0:T(8,128)(2,1)} custom-call(bf16[2,4608,256]{2,1,0:T(8,128)(2,1)} %bitcast.28, s32[12]{0:T(128)} %stack.70.rest_0_.scalars, bf16[2,128,256]{2,1,0:T(8,128)(2,1)} %pad.4.rest_1_.sink_ref, f32[1,256]{1,0:T(1,128)} %bitcast.44, f32[1,1280]{1,0:T(1,128)} %broadcast_in_dim.23.rest_3_.up_scale, ...), custom_call_target="tpu_custom_call" | custom-call | tf_op jit(solution)/shard_map/stage/pallas_call | solution.py:373
  97.4 6.2 %qkv.1 = (bf16[512,256]{1,0:T(8,128)(2,1)}, bf16[2,4608,256]{2,1,0:T(8,128)(2,1)}) custom-call(s32[12]{0:T(128)} %stack.70.rest_0_.scalars, f32[1,256]{1,0:T(1,128)} %bitcast.45, bf16[2,4608,256]{2,1,0:T(8,128)(2,1)} %stage.1.cycle_in, bf16[3,160,256]{2,1,0:T(8,128)(2,1)} %bitcast.39, ...), custom_call_target="tpu_custom_call", output_to_operand_aliasing={{1}: (2, {})} | custom-call | tf_op jit(solution)/shard_map/qkv/pallas_call | solution.py:383
  103.6 5.7 %shard_map.150.refs_1_ = bf16[512,128]{1,0:T(8,128)(2,1)} custom-call(s32[12]{0:T(128)} %stack.70.rest_0_.scalars, bf16[512,256]{1,0:T(8,128)(2,1)} %get-tuple-element.12.query_ref, bf16[2,4608,256]{2,1,0:T(8,128)(2,1)} %get-tuple-element.13.cycle_ref, bf16[2,128,256]{2,1,0:T(8,128)(2,1)} %pad.4.rest_1_.sink_ref), custom_call_target="tpu_custom_call" | custom-call | tf_op jit(solution)/shard_map/pallas_call | solution.py:403
  109.3 5.7 %shard_map.149.refs_0_ = bf16[512,128]{1,0:T(8,128)(2,1)} custom-call(s32[12]{0:T(128)} %stack.70.rest_0_.scalars, bf16[512,256]{1,0:T(8,128)(2,1)} %get-tuple-element.12.query_ref, bf16[2,4608,256]{2,1,0:T(8,128)(2,1)} %get-tuple-element.13.cycle_ref, bf16[2,128,256]{2,1,0:T(8,128)(2,1)} %pad.4.rest_1_.sink_ref), custom_call_target="tpu_custom_call" | custom-call | tf_op jit(solution)/shard_map/pallas_call | solution.py:403
  115.1 2.5 shard_map.151
  118.2 12.8 %collective-permute-start.34 = (bf16[160,640]{1,0:T(8,128)(2,1)}, bf16[160,640]{1,0:T(8,128)(2,1)}, u32[]{:S(2)}, u32[]{:S(2)}) collective-permute-start(bf16[160,640]{1,0:T(8,128)(2,1)} %collective-permute-done.32.refs_6_), channel_id=1, source_target_pairs={{0,6},{1,7},{2,0},{3,1},{4,2},{5,3},{6,4},{7,5},{8,14},{9,15},{10,... | collective-permute-start | bytes 614408 | tf_op jit(solution)/shard_map/ppermute | solution.py:41
  134.7 6.1 %collective-permute-start.28 = (bf16[2,160,640]{2,1,0:T(8,128)(2,1)}, bf16[2,160,640]{2,1,0:T(8,128)(2,1)}, u32[]{:S(2)}, u32[]{:S(2)}) collective-permute-start(bf16[2,160,640]{2,1,0:T(8,128)(2,1)} %pad_maximum_fusion.1.refs_0_), channel_id=1, source_target_pairs={{0,6},{1,7},{2,0},{3,1},{4,2},{5,3},{6,4},{7,5},{8,14},{9,15},{10,... | collective-permute-start | bytes 1228808 | tf_op jit(solution)/shard_map/ppermute | solution.py:41
  140.9 2.5 shard_map.152
  143.4 5.0 %collective-permute-start.22 = (bf16[2,160,1280]{2,1,0:T(8,128)(2,1)}, bf16[2,160,1280]{2,1,0:T(8,128)(2,1)}, u32[]{:S(2)}, u32[]{:S(2)}) collective-permute-start(bf16[2,160,1280]{2,1,0:T(8,128)(2,1)} %collective-permute-done.20.refs_4_), channel_id=1, source_target_pairs={{0,6},{1,7},{2,0},{3,1},{4,2},{5,3},{6,4},{7,5},{8,14},{9,15},{10,... | collective-permute-start | bytes 2457608 | tf_op jit(solution)/shard_map/ppermute | solution.py:41
  152.8 5.0 %collective-permute-done.36.refs_10_ = bf16[160,640]{1,0:T(8,128)(2,1)} collective-permute-done((bf16[160,640]{1,0:T(8,128)(2,1)}, bf16[160,640]{1,0:T(8,128)(2,1)}, u32[]{:S(2)}, u32[]{:S(2)}) %collective-permute-start.36) | collective-permute-done | bytes 204832 | tf_op jit(solution)/shard_map/ppermute | solution.py:41
  161.4 12.6 %collective-permute-done.22.refs_6_ = bf16[2,160,1280]{2,1,0:T(8,128)(2,1)} collective-permute-done((bf16[2,160,1280]{2,1,0:T(8,128)(2,1)}, bf16[2,160,1280]{2,1,0:T(8,128)(2,1)}, u32[]{:S(2)}, u32[]{:S(2)}) %collective-permute-start.22) | collective-permute-done | bytes 819232 | tf_op jit(solution)/shard_map/ppermute | solution.py:41
  176.9 2.3 shard_map.154.refs_10_
  179.1 2.3 shard_map.153.refs_8_.base_ref
  181.4 4.6 %collective-permute-done.29.refs_2_ = bf16[2,160,640]{2,1,0:T(8,128)(2,1)} collective-permute-done((bf16[2,160,640]{2,1,0:T(8,128)(2,1)}, bf16[2,160,640]{2,1,0:T(8,128)(2,1)}, u32[]{:S(2)}, u32[]{:S(2)}) %collective-permute-start.29) | collective-permute-done | bytes 409632 | tf_op jit(solution)/shard_map/ppermute | solution.py:41
  186.0 3.1 %collective-permute-start.30 = (bf16[2,160,640]{2,1,0:T(8,128)(2,1)}, bf16[2,160,640]{2,1,0:T(8,128)(2,1)}, u32[]{:S(2)}, u32[]{:S(2)}) collective-permute-start(bf16[2,160,640]{2,1,0:T(8,128)(2,1)} %collective-permute-done.29.refs_2_), channel_id=1, source_target_pairs={{0,6},{1,7},{2,0},{3,1},{4,2},{5,3},{6,4},{7,5},{8,14},{9,15},{10,... | collective-permute-start | bytes 1228808 | tf_op jit(solution)/shard_map/ppermute | solution.py:41
  191.1 7.2 %collective-permute-done.21.refs_5_ = bf16[2,160,1280]{2,1,0:T(8,128)(2,1)} collective-permute-done((bf16[2,160,1280]{2,1,0:T(8,128)(2,1)}, bf16[2,160,1280]{2,1,0:T(8,128)(2,1)}, u32[]{:S(2)}, u32[]{:S(2)}) %collective-permute-start.21) | collective-permute-done | bytes 819232 | tf_op jit(solution)/shard_map/ppermute | solution.py:49
  198.3 17.6 %collective-permute-done.23.refs_7_ = bf16[2,160,1280]{2,1,0:T(8,128)(2,1)} collective-permute-done((bf16[2,160,1280]{2,1,0:T(8,128)(2,1)}, bf16[2,160,1280]{2,1,0:T(8,128)(2,1)}, u32[]{:S(2)}, u32[]{:S(2)}) %collective-permute-start.23) | collective-permute-done | bytes 819232 | tf_op jit(solution)/shard_map/ppermute | solution.py:49
  215.9 8.7 %units.1.active_ref = bf16[512,1280]{1,0:T(8,128)(2,1)} custom-call(s32[12]{0:T(128)} %stack.70.rest_0_.scalars, f32[1,1280]{1,0:T(1,128)} %broadcast_in_dim.23.rest_3_.up_scale, f32[1,1280]{1,0:T(1,128)} %broadcast_in_dim.24.rest_4_.gate_scale, bf16[2,160,1280]{2,1,0:T(8,128)(2,1)} %copy-done, bf16[2,160,1280]{2,1,0:T(8,128)(2,1)} %collective-permute-done.17.refs_1_, ...), custom_call_target="tpu_custom_call" | custom-call | tf_op jit(solution)/shard_map/units/pallas_call | solution.py:466
  224.7 2.7 %collective-permute-done.35.refs_9_ = bf16[160,640]{1,0:T(8,128)(2,1)} collective-permute-done((bf16[160,640]{1,0:T(8,128)(2,1)}, bf16[160,640]{1,0:T(8,128)(2,1)}, u32[]{:S(2)}, u32[]{:S(2)}) %collective-permute-start.35) | collective-permute-done | bytes 204832 | tf_op jit(solution)/shard_map/ppermute | solution.py:49
  227.3 2.2 collective-permute-done.37.refs_11_
  229.5 4.4 %shard_map.156 = (bf16[128,1280]{1,0:T(8,128)(2,1)}, bf16[128,1280]{1,0:T(8,128)(2,1)}) custom-call(s32[12]{0:T(128)} %stack.70.rest_0_.scalars, bf16[512,1280]{1,0:T(8,128)(2,1)} %units.1.active_ref, bf16[2,160,640]{2,1,0:T(8,128)(2,1)} %pad_maximum_fusion.1.refs_0_, bf16[2,160,640]{2,1,0:T(8,128)(2,1)} %collective-permute-done.28.refs_1_, ...), custom_call_target="tpu_custom_call" | custom-call | tf_op jit(solution)/shard_map/pallas_call | solution.py:485
  233.9 4.4 %shard_map.155 = (bf16[128,1280]{1,0:T(8,128)(2,1)}, bf16[128,1280]{1,0:T(8,128)(2,1)}) custom-call(s32[12]{0:T(128)} %stack.70.rest_0_.scalars, bf16[512,1280]{1,0:T(8,128)(2,1)} %units.1.active_ref, bf16[2,160,640]{2,1,0:T(8,128)(2,1)} %pad_maximum_fusion.1.refs_0_, bf16[2,160,640]{2,1,0:T(8,128)(2,1)} %collective-permute-done.28.refs_1_, ...), custom_call_target="tpu_custom_call" | custom-call | tf_op jit(solution)/shard_map/pallas_call | solution.py:485
  240.6 9.2 %collective-permute-done.40.refs_2_ = bf16[128,1280]{1,0:T(8,128)(2,1)} collective-permute-done((bf16[128,1280]{1,0:T(8,128)(2,1)S(1)}, bf16[128,1280]{1,0:T(8,128)(2,1)}, u32[]{:S(2)}, u32[]{:S(2)}) %collective-permute-start.40) | collective-permute-done | bytes 327712 | tf_op jit(solution)/shard_map/ppermute | solution.py:55
  249.8 2.4 shard_map.157
  (101 shorter events, 40.9 us)
Async XLA Ops:
  2.7 45.8 %collective-permute-start.18 = (bf16[2,160,1280]{2,1,0:T(8,128)(2,1)S(1)}, bf16[2,160,1280]{2,1,0:T(8,128)(2,1)}, u32[]{:S(2)}, u32[]{:S(2)}) collective-permute-start(bf16[2,160,1280]{2,1,0:T(8,128)(2,1)S(1)} %pad_maximum_fusion.refs_0_), channel_id=1, source_target_pairs={{0,6},{1,7},{2,0},{3,1},{4,2},{5,3},{6,4},{7,5},{8,14},{9,15},{10,... | collective-permute-start | bytes 2457608 | tf_op jit(solution)/shard_map/ppermute | solution.py:41
  7.8 22.9 %collective-permute-start.1 = (bf16[3,160,256]{2,1,0:T(8,128)(2,1)}, bf16[3,160,256]{2,1,0:T(8,128)(2,1)S(1)}, u32[]{:S(2)}, u32[]{:S(2)}) collective-permute-start(bf16[3,160,256]{2,1,0:T(8,128)(2,1)} %bitcast.37), channel_id=1, source_target_pairs={{0,6},{1,7},{2,0},{3,1},{4,2},{5,3},{6,4},{7,5},{8,14},{9,15},{10,... | collective-permute-start | bytes 737288 | tf_op jit(solution)/shard_map/ppermute | solution.py:41
  8.3 27.5 %collective-permute-start = (bf16[3,160,256]{2,1,0:T(8,128)(2,1)}, bf16[3,160,256]{2,1,0:T(8,128)(2,1)S(1)}, u32[]{:S(2)}, u32[]{:S(2)}) collective-permute-start(bf16[3,160,256]{2,1,0:T(8,128)(2,1)} %bitcast.38), channel_id=1, source_target_pairs={{0,1},{1,0},{2,3},{3,2},{4,5},{5,4},{6,7},{7,6},{8,9},{9,8},{10,11... | collective-permute-start | bytes 737288 | tf_op jit(solution)/shard_map/ppermute | solution.py:49
  10.3 38.3 %collective-permute-start.8 = (bf16[128,1280]{1,0:T(8,128)(2,1)}, bf16[128,1280]{1,0:T(8,128)(2,1)S(1)}, u32[]{:S(2)}, u32[]{:S(2)}) collective-permute-start(bf16[128,1280]{1,0:T(8,128)(2,1)} %bitcast.29), channel_id=1, source_target_pairs={{0,16},{8,24},{16,0},{24,8},{1,17},{9,25},{17,1},{25,9},{2,18},{10... | collective-permute-start | bytes 983048 | tf_op jit(solution)/shard_map/ppermute | solution.py:55
  17.4 31.3 %collective-permute-start.7 = (bf16[128,1280]{1,0:T(8,128)(2,1)}, bf16[128,1280]{1,0:T(8,128)(2,1)S(1)}, u32[]{:S(2)}, u32[]{:S(2)}) collective-permute-start(bf16[128,1280]{1,0:T(8,128)(2,1)} %bitcast.30), channel_id=1, source_target_pairs={{0,8},{8,0},{16,24},{24,16},{1,9},{9,1},{17,25},{25,17},{2,10},{10... | collective-permute-start | bytes 983048 | tf_op jit(solution)/shard_map/ppermute | solution.py:59
  30.7 13.6 %collective-permute-start.3 = (bf16[3,160,256]{2,1,0:T(8,128)(2,1)S(1)}, bf16[3,160,256]{2,1,0:T(8,128)(2,1)}, u32[]{:S(2)}, u32[]{:S(2)}) collective-permute-start(bf16[3,160,256]{2,1,0:T(8,128)(2,1)S(1)} %collective-permute-done.1.rest_2_), channel_id=1, source_target_pairs={{0,6},{1,7},{2,0},{3,1},{4,2},{5,3},{6,4},{7,5},{8,14},{9,15},{10,... | collective-permute-start | bytes 737288 | tf_op jit(solution)/shard_map/ppermute | solution.py:41
  42.7 34.8 %collective-permute-start.2 = (bf16[3,160,256]{2,1,0:T(8,128)(2,1)S(1)}, bf16[3,160,256]{2,1,0:T(8,128)(2,1)S(1)}, u32[]{:S(2)}, u32[]{:S(2)}) collective-permute-start(bf16[3,160,256]{2,1,0:T(8,128)(2,1)S(1)} %collective-permute-done.1.rest_2_), channel_id=1, source_target_pairs={{0,1},{1,0},{2,3},{3,2},{4,5},{5,4},{6,7},{7,6},{8,9},{9,8},{10,11... | collective-permute-start | bytes 737288 | tf_op jit(solution)/shard_map/ppermute | solution.py:49
  44.3 34.0 %collective-permute-start.5 = (bf16[3,160,256]{2,1,0:T(8,128)(2,1)}, bf16[3,160,256]{2,1,0:T(8,128)(2,1)}, u32[]{:S(2)}, u32[]{:S(2)}) collective-permute-start(bf16[3,160,256]{2,1,0:T(8,128)(2,1)} %collective-permute-done.3.rest_4_), channel_id=1, source_target_pairs={{0,6},{1,7},{2,0},{3,1},{4,2},{5,3},{6,4},{7,5},{8,14},{9,15},{10,... | collective-permute-start | bytes 737288 | tf_op jit(solution)/shard_map/ppermute | solution.py:41
  48.5 94.8 %collective-permute-start.20 = (bf16[2,160,1280]{2,1,0:T(8,128)(2,1)}, bf16[2,160,1280]{2,1,0:T(8,128)(2,1)}, u32[]{:S(2)}, u32[]{:S(2)}) collective-permute-start(bf16[2,160,1280]{2,1,0:T(8,128)(2,1)} %collective-permute-done.18.refs_2_), channel_id=1, source_target_pairs={{0,6},{1,7},{2,0},{3,1},{4,2},{5,3},{6,4},{7,5},{8,14},{9,15},{10,... | collective-permute-start | bytes 2457608 | tf_op jit(solution)/shard_map/ppermute | solution.py:41
  48.6 24.5 %collective-permute-start.12 = (bf16[2,160,256]{2,1,0:T(8,128)(2,1)S(1)}, bf16[2,160,256]{2,1,0:T(8,128)(2,1)}, u32[]{:S(2)}, u32[]{:S(2)}) collective-permute-start(bf16[2,160,256]{2,1,0:T(8,128)(2,1)S(1)} %collective-permute-done.11.refs_3_), channel_id=1, source_target_pairs={{0,6},{1,7},{2,0},{3,1},{4,2},{5,3},{6,4},{7,5},{8,14},{9,15},{10,... | collective-permute-start | bytes 491528 | tf_op jit(solution)/shard_map/ppermute | solution.py:41
  49.4 32.2 %collective-permute-start.9 = (bf16[128,1280]{1,0:T(8,128)(2,1)S(1)}, bf16[128,1280]{1,0:T(8,128)(2,1)S(1)}, u32[]{:S(2)}, u32[]{:S(2)}) collective-permute-start(bf16[128,1280]{1,0:T(8,128)(2,1)S(1)} %collective-permute-done.8.rest_10_.base_ref), channel_id=1, source_target_pairs={{0,8},{8,0},{16,24},{24,16},{1,9},{9,1},{17,25},{25,17},{2,10},{10... | collective-permute-start | bytes 983048 | tf_op jit(solution)/shard_map/ppermute | solution.py:59
  73.1 41.9 %collective-permute-start.13 = (bf16[2,160,256]{2,1,0:T(8,128)(2,1)}, bf16[2,160,256]{2,1,0:T(8,128)(2,1)}, u32[]{:S(2)}, u32[]{:S(2)}) collective-permute-start(bf16[2,160,256]{2,1,0:T(8,128)(2,1)} %collective-permute-done.12.refs_4_), channel_id=1, source_target_pairs={{0,6},{1,7},{2,0},{3,1},{4,2},{5,3},{6,4},{7,5},{8,14},{9,15},{10,... | collective-permute-start | bytes 491528 | tf_op jit(solution)/shard_map/ppermute | solution.py:41
  77.6 19.9 %collective-permute-start.4 = (bf16[3,160,256]{2,1,0:T(8,128)(2,1)}, bf16[3,160,256]{2,1,0:T(8,128)(2,1)}, u32[]{:S(2)}, u32[]{:S(2)}) collective-permute-start(bf16[3,160,256]{2,1,0:T(8,128)(2,1)} %collective-permute-done.3.rest_4_), channel_id=1, source_target_pairs={{0,1},{1,0},{2,3},{3,2},{4,5},{5,4},{6,7},{7,6},{8,9},{9,8},{10,11... | collective-permute-start | bytes 737288 | tf_op jit(solution)/shard_map/ppermute | solution.py:49
  78.3 19.2 %collective-permute-start.6 = (bf16[3,160,256]{2,1,0:T(8,128)(2,1)}, bf16[3,160,256]{2,1,0:T(8,128)(2,1)}, u32[]{:S(2)}, u32[]{:S(2)}) collective-permute-start(bf16[3,160,256]{2,1,0:T(8,128)(2,1)} %collective-permute-done.5.rest_6_), channel_id=1, source_target_pairs={{0,1},{1,0},{2,3},{3,2},{4,5},{5,4},{6,7},{7,6},{8,9},{9,8},{10,11... | collective-permute-start | bytes 737288 | tf_op jit(solution)/shard_map/ppermute | solution.py:49
  82.3 35.8 %collective-permute-start.32 = (bf16[160,640]{1,0:T(8,128)(2,1)}, bf16[160,640]{1,0:T(8,128)(2,1)}, u32[]{:S(2)}, u32[]{:S(2)}) collective-permute-start(bf16[160,640]{1,0:T(8,128)(2,1)} %get-tuple-element.22.refs_4_), channel_id=1, source_target_pairs={{0,6},{1,7},{2,0},{3,1},{4,2},{5,3},{6,4},{7,5},{8,14},{9,15},{10,... | collective-permute-start | bytes 614408 | tf_op jit(solution)/shard_map/ppermute | solution.py:41
  117.6 25.8 %collective-permute-start.14 = (bf16[128,1280]{1,0:T(8,128)(2,1)}, bf16[128,1280]{1,0:T(8,128)(2,1)}, u32[]{:S(2)}, u32[]{:S(2)}) collective-permute-start(bf16[128,1280]{1,0:T(8,128)(2,1)} %get-tuple-element.15), channel_id=1, source_target_pairs={{0,8},{8,0},{16,24},{24,16},{1,9},{9,1},{17,25},{25,17},{2,10},{10... | collective-permute-start | bytes 983048 | tf_op jit(solution)/shard_map/ppermute | solution.py:59
  117.6 15.3 %collective-permute-start.27 = (bf16[160,640]{1,0:T(8,128)(2,1)}, bf16[160,640]{1,0:T(8,128)(2,1)S(1)}, u32[]{:S(2)}, u32[]{:S(2)}) collective-permute-start(bf16[160,640]{1,0:T(8,128)(2,1)} %get-tuple-element.24), channel_id=1, source_target_pairs={{0,1},{1,0},{2,3},{3,2},{4,5},{5,4},{6,7},{7,6},{8,9},{9,8},{10,11... | collective-permute-start | bytes 614408 | tf_op jit(solution)/shard_map/ppermute | solution.py:49
  118.2 22.7 %collective-permute-start.34 = (bf16[160,640]{1,0:T(8,128)(2,1)}, bf16[160,640]{1,0:T(8,128)(2,1)}, u32[]{:S(2)}, u32[]{:S(2)}) collective-permute-start(bf16[160,640]{1,0:T(8,128)(2,1)} %collective-permute-done.32.refs_6_), channel_id=1, source_target_pairs={{0,6},{1,7},{2,0},{3,1},{4,2},{5,3},{6,4},{7,5},{8,14},{9,15},{10,... | collective-permute-start | bytes 614408 | tf_op jit(solution)/shard_map/ppermute | solution.py:41
  130.9 50.5 %collective-permute-start.17 = (bf16[2,160,1280]{2,1,0:T(8,128)(2,1)}, bf16[2,160,1280]{2,1,0:T(8,128)(2,1)}, u32[]{:S(2)}, u32[]{:S(2)}) collective-permute-start(bf16[2,160,1280]{2,1,0:T(8,128)(2,1)} %copy-done), channel_id=1, source_target_pairs={{0,1},{1,0},{2,3},{3,2},{4,5},{5,4},{6,7},{7,6},{8,9},{9,8},{10,11... | collective-permute-start | bytes 2457608 | tf_op jit(solution)/shard_map/ppermute | solution.py:49
  134.7 24.6 %collective-permute-start.28 = (bf16[2,160,640]{2,1,0:T(8,128)(2,1)}, bf16[2,160,640]{2,1,0:T(8,128)(2,1)}, u32[]{:S(2)}, u32[]{:S(2)}) collective-permute-start(bf16[2,160,640]{2,1,0:T(8,128)(2,1)} %pad_maximum_fusion.1.refs_0_), channel_id=1, source_target_pairs={{0,6},{1,7},{2,0},{3,1},{4,2},{5,3},{6,4},{7,5},{8,14},{9,15},{10,... | collective-permute-start | bytes 1228808 | tf_op jit(solution)/shard_map/ppermute | solution.py:41
  140.8 17.0 %collective-permute-start.36 = (bf16[160,640]{1,0:T(8,128)(2,1)}, bf16[160,640]{1,0:T(8,128)(2,1)}, u32[]{:S(2)}, u32[]{:S(2)}) collective-permute-start(bf16[160,640]{1,0:T(8,128)(2,1)} %collective-permute-done.34.refs_8_), channel_id=1, source_target_pairs={{0,6},{1,7},{2,0},{3,1},{4,2},{5,3},{6,4},{7,5},{8,14},{9,15},{10,... | collective-permute-start | bytes 614408 | tf_op jit(solution)/shard_map/ppermute | solution.py:41
  143.4 30.6 %collective-permute-start.22 = (bf16[2,160,1280]{2,1,0:T(8,128)(2,1)}, bf16[2,160,1280]{2,1,0:T(8,128)(2,1)}, u32[]{:S(2)}, u32[]{:S(2)}) collective-permute-start(bf16[2,160,1280]{2,1,0:T(8,128)(2,1)} %collective-permute-done.20.refs_4_), channel_id=1, source_target_pairs={{0,6},{1,7},{2,0},{3,1},{4,2},{5,3},{6,4},{7,5},{8,14},{9,15},{10,... | collective-permute-start | bytes 2457608 | tf_op jit(solution)/shard_map/ppermute | solution.py:41
  157.9 16.7 %collective-permute-start.16 = (bf16[128,1280]{1,0:T(8,128)(2,1)S(1)}, bf16[128,1280]{1,0:T(8,128)(2,1)S(1)}, u32[]{:S(2)}, u32[]{:S(2)}) collective-permute-start(bf16[128,1280]{1,0:T(8,128)(2,1)S(1)} %add_convert_fusion.1.refs_0_), channel_id=1, source_target_pairs={{0,16},{8,24},{16,0},{24,8},{1,17},{9,25},{17,1},{25,9},{2,18},{10... | collective-permute-start | bytes 983048 | tf_op jit(solution)/shard_map/ppermute | solution.py:55
  159.3 26.7 %collective-permute-start.19 = (bf16[2,160,1280]{2,1,0:T(8,128)(2,1)}, bf16[2,160,1280]{2,1,0:T(8,128)(2,1)}, u32[]{:S(2)}, u32[]{:S(2)}) collective-permute-start(bf16[2,160,1280]{2,1,0:T(8,128)(2,1)} %collective-permute-done.18.refs_2_), channel_id=1, source_target_pairs={{0,1},{1,0},{2,3},{3,2},{4,5},{5,4},{6,7},{7,6},{8,9},{9,8},{10,11... | collective-permute-start | bytes 2457608 | tf_op jit(solution)/shard_map/ppermute | solution.py:49
  160.8 37.5 %collective-permute-start.21 = (bf16[2,160,1280]{2,1,0:T(8,128)(2,1)}, bf16[2,160,1280]{2,1,0:T(8,128)(2,1)}, u32[]{:S(2)}, u32[]{:S(2)}) collective-permute-start(bf16[2,160,1280]{2,1,0:T(8,128)(2,1)} %collective-permute-done.20.refs_4_), channel_id=1, source_target_pairs={{0,1},{1,0},{2,3},{3,2},{4,5},{5,4},{6,7},{7,6},{8,9},{9,8},{10,11... | collective-permute-start | bytes 2457608 | tf_op jit(solution)/shard_map/ppermute | solution.py:49
  174.0 41.9 %collective-permute-start.23 = (bf16[2,160,1280]{2,1,0:T(8,128)(2,1)}, bf16[2,160,1280]{2,1,0:T(8,128)(2,1)}, u32[]{:S(2)}, u32[]{:S(2)}) collective-permute-start(bf16[2,160,1280]{2,1,0:T(8,128)(2,1)} %collective-permute-done.22.refs_6_), channel_id=1, source_target_pairs={{0,1},{1,0},{2,3},{3,2},{4,5},{5,4},{6,7},{7,6},{8,9},{9,8},{10,11... | collective-permute-start | bytes 2457608 | tf_op jit(solution)/shard_map/ppermute | solution.py:49
  175.3 10.7 %collective-permute-start.29 = (bf16[2,160,640]{2,1,0:T(8,128)(2,1)}, bf16[2,160,640]{2,1,0:T(8,128)(2,1)}, u32[]{:S(2)}, u32[]{:S(2)}) collective-permute-start(bf16[2,160,640]{2,1,0:T(8,128)(2,1)} %collective-permute-done.28.refs_1_), channel_id=1, source_target_pairs={{0,6},{1,7},{2,0},{3,1},{4,2},{5,3},{6,4},{7,5},{8,14},{9,15},{10,... | collective-permute-start | bytes 1228808 | tf_op jit(solution)/shard_map/ppermute | solution.py:41
  186.0 43.5 %collective-permute-start.30 = (bf16[2,160,640]{2,1,0:T(8,128)(2,1)}, bf16[2,160,640]{2,1,0:T(8,128)(2,1)}, u32[]{:S(2)}, u32[]{:S(2)}) collective-permute-start(bf16[2,160,640]{2,1,0:T(8,128)(2,1)} %collective-permute-done.29.refs_2_), channel_id=1, source_target_pairs={{0,6},{1,7},{2,0},{3,1},{4,2},{5,3},{6,4},{7,5},{8,14},{9,15},{10,... | collective-permute-start | bytes 1228808 | tf_op jit(solution)/shard_map/ppermute | solution.py:41
  189.1 35.6 %collective-permute-start.31 = (bf16[160,640]{1,0:T(8,128)(2,1)}, bf16[160,640]{1,0:T(8,128)(2,1)}, u32[]{:S(2)}, u32[]{:S(2)}) collective-permute-start(bf16[160,640]{1,0:T(8,128)(2,1)} %get-tuple-element.22.refs_4_), channel_id=1, source_target_pairs={{0,1},{1,0},{2,3},{3,2},{4,5},{5,4},{6,7},{7,6},{8,9},{9,8},{10,11... | collective-permute-start | bytes 614408 | tf_op jit(solution)/shard_map/ppermute | solution.py:49
  190.0 34.7 %collective-permute-start.33 = (bf16[160,640]{1,0:T(8,128)(2,1)}, bf16[160,640]{1,0:T(8,128)(2,1)}, u32[]{:S(2)}, u32[]{:S(2)}) collective-permute-start(bf16[160,640]{1,0:T(8,128)(2,1)} %collective-permute-done.32.refs_6_), channel_id=1, source_target_pairs={{0,1},{1,0},{2,3},{3,2},{4,5},{5,4},{6,7},{7,6},{8,9},{9,8},{10,11... | collective-permute-start | bytes 614408 | tf_op jit(solution)/shard_map/ppermute | solution.py:49
  198.3 29.0 %collective-permute-start.35 = (bf16[160,640]{1,0:T(8,128)(2,1)}, bf16[160,640]{1,0:T(8,128)(2,1)}, u32[]{:S(2)}, u32[]{:S(2)}) collective-permute-start(bf16[160,640]{1,0:T(8,128)(2,1)} %collective-permute-done.34.refs_8_), channel_id=1, source_target_pairs={{0,1},{1,0},{2,3},{3,2},{4,5},{5,4},{6,7},{7,6},{8,9},{9,8},{10,11... | collective-permute-start | bytes 614408 | tf_op jit(solution)/shard_map/ppermute | solution.py:49
  215.9 13.6 %collective-permute-start.37 = (bf16[160,640]{1,0:T(8,128)(2,1)}, bf16[160,640]{1,0:T(8,128)(2,1)}, u32[]{:S(2)}, u32[]{:S(2)}) collective-permute-start(bf16[160,640]{1,0:T(8,128)(2,1)} %collective-permute-done.36.refs_10_), channel_id=1, source_target_pairs={{0,1},{1,0},{2,3},{3,2},{4,5},{5,4},{6,7},{7,6},{8,9},{9,8},{10,11... | collective-permute-start | bytes 614408 | tf_op jit(solution)/shard_map/ppermute | solution.py:49
  (22 other events, 218.0 us)

commit v2 on v1

--- a/solution.py
+++ b/solution.py
@@ -20,6 +20,7 @@
 SMEM = pl.BlockSpec(memory_space=pltpu.SMEM)
 ANY = pl.BlockSpec(memory_space=pl.ANY)
 PARAMS = pltpu.CompilerParams(vmem_limit_bytes=67043328)
+LIGHT = pltpu.CompilerParams(vmem_limit_bytes=24 << 20)
 
 
 class Layout:
@@ -140,12 +141,12 @@
     target[...] = source[...]
 
 
-def norm_kernel(base_ref, alpha_ref, *refs):
+def norm_kernel(row, base_ref, alpha_ref, *refs):
     terms, out_ref = refs[:-1], refs[-1]
     change = terms[0][...].astype(jnp.float32)
     for term in terms[1:]:
         change += term[...].astype(jnp.float32)
-    out_ref[...] = step_towards(base_ref[...].astype(jnp.float32), change, alpha_ref[...])
+    out_ref[...] = step_towards(base_ref[...].astype(jnp.float32), change, alpha_ref[row : row + 1, :])
 
 
 def qkv_kernel(spots, count, blocks, own_rows, scalars, scale_ref, cycle_in, *rest):
@@ -209,7 +210,7 @@
         store.wait()
 
 
-def attention_kernel(own_rows, scalars, query_ref, cycle_ref, sink_ref, out_ref, scores, bias):
+def attention_kernel(own_rows, scalars, query_ref, cycle_ref, sink_ref, out_ref, pair, bias):
     length, x, c, nx = scalars[0], scalars[1], scalars[2], scalars[3]
     new_count, lanes = query_ref.shape
     cycle_size = cycle_ref.shape[1]
@@ -217,6 +218,7 @@
     sink_lane = lax.broadcasted_iota(jnp.int32, (1, sink_ref.shape[1]), 1)
     sink_bias = jnp.where(sink_lane < SINK, 0.0, NEG)
     contract = (((1,), (1,)), ((), ()))
+    scores = pair.at[0]
 
     def run(keys):
         sizes = [min(CHUNK, keys - at) for at in range(0, keys, CHUNK)]
@@ -236,7 +238,7 @@
                 ahead = jnp.where(lagging >= 0, SINK + slot + turn - length, 1 << 20)
                 lag = moment - ahead
                 seen = (lag >= 0) & (lag < WINDOW)
-                bias[:, begin : begin + size] = jnp.where(seen, 0.0, NEG)
+                bias[0, :, begin : begin + size] = jnp.where(seen, 0.0, NEG)
             result = jnp.zeros((own_rows, lanes), jnp.float32)
             for head in range(lanes // HD):
                 mine = lane_head == head
@@ -255,7 +257,7 @@
                         contract,
                         preferred_element_type=jnp.float32,
                     )
-                    part = part + bias[:, begin : begin + size]
+                    part = part + bias[0, :, begin : begin + size]
                     scores[:, begin : begin + size] = part
                     highest = jnp.maximum(highest, jnp.max(part, axis=-1, keepdims=True))
                 weights = jnp.exp(sink_scores - highest)
@@ -277,36 +279,132 @@
 
         lax.fori_loop(0, new_count // own_rows, tile, 0)
 
+    def run_full():
+        start = lax.rem(length - SINK, cycle_size)
+        chunks = cycle_size // CHUNK
+        masked = min((2 * new_count + CHUNK - 1) // CHUNK + 1, chunks)
+        firsts = [
+            pl.multiple_of(lax.rem(start // CHUNK + n, chunks) * CHUNK, CHUNK) for n in range(chunks)
+        ]
+        steps = [(i, head) for i in range(new_count // own_rows) for head in range(lanes // HD)]
+        queries, highest, results = {}, {}, {}
+
+        def masks(i):
+            from_x = lax.rem(x - i // 2 + nx, nx)
+            from_c = 1 - c if i % 2 == 1 else c
+            moment = (from_x * 2 + from_c) * own_rows + lax.broadcasted_iota(
+                jnp.int32, (own_rows, 1), 0
+            )
+            for n in range(masked):
+                slot = firsts[n] + lax.broadcasted_iota(jnp.int32, (1, CHUNK), 1)
+                since = slot - start
+                since = jnp.where(since < 0, since + cycle_size, since)
+                ahead = jnp.where(since < new_count, since, since - cycle_size)
+                lag = moment - ahead
+                seen = (lag >= 0) & (lag < WINDOW)
+                bias[i % 2, :, n * CHUNK : (n + 1) * CHUNK] = jnp.where(seen, 0.0, NEG)
+
+        def score_sinks(u):
+            i, head = steps[u]
+            rows = query_ref[i * own_rows : (i + 1) * own_rows, :].astype(jnp.float32)
+            queries[u] = jnp.where(lane_head == head, rows, 0.0).astype(jnp.bfloat16)
+            sink = (
+                lax.dot_general(
+                    queries[u], sink_ref[0], contract, preferred_element_type=jnp.float32
+                )
+                + sink_bias
+            )
+            highest[u] = [sink]
+            return sink
+
+        def score(u, n):
+            part = lax.dot_general(
+                queries[u],
+                cycle_ref[0, pl.ds(firsts[n], CHUNK), :],
+                contract,
+                preferred_element_type=jnp.float32,
+            )
+            if n < masked:
+                part = part + bias[steps[u][0] % 2, :, n * CHUNK : (n + 1) * CHUNK]
+            pair[u % 2, :, n * CHUNK : (n + 1) * CHUNK] = part
+            for lane in range(0, CHUNK, 128):
+                highest[u].append(part[:, lane : lane + 128])
+            while len(highest[u]) > 1:
+                highest[u] = [
+                    jnp.maximum(a, b) for a, b in zip(highest[u][::2], highest[u][1::2])
+                ] + highest[u][len(highest[u]) // 2 * 2 :]
+
+        sinks = {}
+
+        def begin(u):
+            if steps[u][1] == 0:
+                masks(steps[u][0])
+            sinks[u] = score_sinks(u)
+
+        begin(0)
+        for n in range(chunks):
+            score(0, n)
+        for u, (i, head) in enumerate(steps):
+            top = jnp.max(highest[u][0], axis=-1, keepdims=True)
+            weights = jnp.exp(sinks[u] - top)
+            lanes_total = weights
+            summed = jnp.dot(
+                weights.astype(jnp.bfloat16), sink_ref[1], preferred_element_type=jnp.float32
+            )
+            if u + 1 < len(steps):
+                begin(u + 1)
+            for n in range(chunks):
+                if u + 1 < len(steps):
+                    score(u + 1, n)
+                weights = jnp.exp(pair[u % 2, :, n * CHUNK : (n + 1) * CHUNK] - top)
+                for lane in range(0, CHUNK, 128):
+                    lanes_total = lanes_total + weights[:, lane : lane + 128]
+                summed += jnp.dot(
+                    weights.astype(jnp.bfloat16),
+                    cycle_ref[1, pl.ds(firsts[n], CHUNK), :],
+                    preferred_element_type=jnp.float32,
+                )
+            total = jnp.sum(lanes_total, axis=-1, keepdims=True)
+            before = results.get(i, jnp.zeros((own_rows, lanes), jnp.float32))
+            results[i] = jnp.where(lane_head == head, summed / total, before)
+            if head == lanes // HD - 1:
+                out_ref[i * own_rows : (i + 1) * own_rows, :] = results[i].astype(jnp.bfloat16)
+
     few = length + new_count - SINK <= SHORT_KEYS
+    full = length - SINK >= cycle_size
 
     @pl.when(few)
     def _():
         run(SHORT_KEYS)
 
-    @pl.when(jnp.logical_not(few))
+    @pl.when(full)
+    def _():
+        run_full()
+
+    @pl.when(jnp.logical_not(few | full))
     def _():
         run(cycle_size)
 
 
-def mix_kernel(spots, count, parts, own_rows, rows, scalars, *refs):
+def mix_kernel(spots, count, parts, own_rows, scalars, *refs):
     attended, pieces = refs[:parts], refs[parts : parts + count]
     kept_ref, sent_ref, held = refs[parts + count :]
     place(scalars, pieces, spots, held)
-    wide = jnp.concatenate([ref[rows, :] for ref in attended], axis=1)
+    wide = jnp.concatenate([ref[...] for ref in attended], axis=1)
     mixed = lax.dot_general(
         wide, held[...], (((1,), (1,)), ((), ())), preferred_element_type=jnp.float32
     ).astype(jnp.bfloat16)
     split_rows(mixed, kept_ref, sent_ref, own_rows)
 
 
-def units_kernel(spots, count, blocks, scalars, up_scale, gate_scale, *refs):
+def units_kernel(spots, count, blocks, scalars, scale_ref, *refs):
     pieces, row_refs = refs[:count], refs[count : count + blocks]
     out_ref, held = refs[count + blocks :]
     rows = jnp.concatenate([ref[...] for ref in row_refs], axis=0)
     for plane in range(2):
         place(scalars, pieces, spots, held.at[plane], (plane,))
-    up = jnp.dot(rows, held[0], preferred_element_type=jnp.float32) * up_scale[...]
-    gate = jnp.dot(rows, held[1], preferred_element_type=jnp.float32) * gate_scale[...]
+    up = jnp.dot(rows, held[0], preferred_element_type=jnp.float32) * scale_ref[:1, :]
+    gate = jnp.dot(rows, held[1], preferred_element_type=jnp.float32) * scale_ref[1:, :]
     out_ref[...] = (up * (gate / (1.0 + jnp.exp(-gate)))).astype(jnp.bfloat16)
 
 
@@ -367,9 +465,9 @@
 
     scalars = jnp.stack([lengths[0], here.x, here.c, jnp.int32(nx), *here.blocks()])
     sinks = jnp.pad(sink_kv[0], ((0, 0), (0, 128 - SINK), (0, 0)))
-    vectors = [s_qk[None], s_up[None], s_gate[None], alpha_attn[None], alpha_mlp[None]]
-    early = [scalars, sinks, *vectors]
-    scale_qk, scale_up, scale_gate, alpha_attn, alpha_mlp = vectors
+    scale_qk, scales = s_qk[None], jnp.stack([s_up, s_gate])
+    alphas = jnp.stack([alpha_attn, alpha_mlp])
+    early = [scalars, sinks, scale_qk, scales, alphas]
     staged = pl.pallas_call(
         stage_kernel,
         grid=(9,),
@@ -412,8 +510,8 @@
             ],
             out_specs=pl.BlockSpec((new_count, lanes), lambda _: (0, 0)),
             scratch_shapes=[
-                pltpu.VMEM((own_rows, cycle_size), jnp.float32),
-                pltpu.VMEM((own_rows, cycle_size), jnp.float32),
+                pltpu.VMEM((2, own_rows, cycle_size), jnp.float32),
+                pltpu.VMEM((2, own_rows, cycle_size), jnp.float32),
             ],
             compiler_params=PARAMS,
         )(scalars, queries, new_cycle, sinks)
@@ -426,39 +524,37 @@
         size = (rows.stop - rows.start) // 2
         return (jax.ShapeDtypeStruct((size, model_width), jnp.bfloat16),) * 2
 
-    def mix(group):
-        rows = groups[group]
+    def mix():
         return pl.pallas_call(
-            functools.partial(mix_kernel, out_spots, len(out_arrays), parts, own_rows, rows),
-            out_shape=halves(rows),
+            functools.partial(mix_kernel, out_spots, len(out_arrays), parts, own_rows),
+            out_shape=halves(slice(0, new_count)),
             in_specs=[SMEM] + [VMEM] * (parts + len(out_arrays)),
             out_specs=(VMEM, VMEM),
             scratch_shapes=[pltpu.VMEM((model_width, local_cols), jnp.bfloat16)],
             compiler_params=PARAMS,
+            name="mix",
         )(scalars, *attended, *out_arrays)
 
-    far = here.core_sum(mix("a"))
-    near = here.core_sum(mix("b"))
-    sums = [part.astype(jnp.bfloat16) for part in [near, *jnp.split(far, nx - 1)]]
+    sums = jnp.split(here.core_sum(mix()).astype(jnp.bfloat16), nx)
     totals = [[part] for part in sums]
     for step in range(1, nx):
         for d in reversed(range(nx)):
             moved = here.to_x(sums[d], step)
             totals[(d + step) % nx].append(moved)
 
-    def norm(base, alpha, terms):
+    def norm(base, row, terms, name):
         return pl.pallas_call(
-            norm_kernel,
+            functools.partial(norm_kernel, row),
             out_shape=jax.ShapeDtypeStruct(base.shape, jnp.bfloat16),
             in_specs=[VMEM] * (2 + len(terms)),
             out_specs=VMEM,
-            compiler_params=PARAMS,
-        )(base, alpha, *terms)
+            compiler_params=LIGHT if name == "last" else PARAMS,
+        )(base, alphas, *terms)
 
     after = []
     after_blocks = []
     for d in range(nx):
-        after.append(norm(row_blocks[2 * d], alpha_attn, totals[d]))
+        after.append(norm(row_blocks[2 * d], 0, totals[d], f"norm{d}"))
         after_blocks += [after[d], here.swap_core(after[d])]
 
     tile = 256 if units % 256 == 0 else 128
@@ -468,14 +564,14 @@
         grid=(units // tile,),
         out_shape=jax.ShapeDtypeStruct((new_count, units), jnp.bfloat16),
         in_specs=[SMEM]
-        + [pl.BlockSpec((1, tile), lambda n: (0, n))] * 2
+        + [pl.BlockSpec((2, tile), lambda n: (0, n))]
         + [pl.BlockSpec((2, piece_rows, tile), lambda n: (0, 0, n))] * len(gated_arrays)
         + [pl.BlockSpec((own_rows, model_width), lambda n: (0, 0))] * blocks,
         out_specs=pl.BlockSpec((new_count, tile), lambda n: (0, n)),
         scratch_shapes=[pltpu.VMEM((2, model_width, tile), jnp.bfloat16)],
         compiler_params=PARAMS,
         name="units",
-    )(scalars, scale_up, scale_gate, *gated_arrays, *after_blocks)
+    )(scalars, scales, *gated_arrays, *after_blocks)
 
     down_arrays = [*first_arrays, *second_arrays]
 
@@ -488,14 +584,14 @@
             in_specs=[SMEM] + [VMEM] * (1 + len(down_arrays)),
             out_specs=(VMEM, VMEM),
             scratch_shapes=[pltpu.VMEM((model_width, units), jnp.bfloat16)],
-            compiler_params=PARAMS,
+            compiler_params=LIGHT,
         )(scalars, active, *down_arrays)
 
     far = jnp.split(here.core_sum(lower("a")).astype(jnp.bfloat16), nx - 1)
     kept, sent = lower("b")
     terms = [kept, here.swap_core(sent)]
     terms += [here.to_x(far[d - 1], -d) for d in range(1, nx)]
-    result = norm(after[0], alpha_mlp, terms)
+    result = norm(after[0], 1, terms, "last")
     return (result[None], new_cycle[None])
 
 

time: 253 us -> 221 us (0.87)
  waiting for transfers between devices: 112 us -> 94.5 us
  Pallas kernels: 54.5 us -> 48.4 us
  other arithmetic: 7.27 us -> 2.71 us
  starting transfers between devices: 64 us -> 60.8 us
    ppermute x15, waiting for transfers between devices: 66.1 us -> 57.3 us  [from_z(): return lax.ppermute(value, 'gy', pairs)]
    ppermute x14, waiting for transfers between devices: 35.2 us -> 28.4 us  [from_y(): return lax.ppermute(value, 'gy', pairs)]
    unnamed x26 -> x76, local copies, waits for them, and re-layouts: 3.9 us -> 9.06 us
    broadcast_in_dim x4 -> x0, local copies, waits for them, and re-layouts: 5.14 us -> none  [the longest x1 1.3 us: per_device(): alpha_attn[None]]
    pallas_call x2, Pallas kernels: 8.82 us -> 5.81 us  [lower(): pl.pallas_call(functools.partial(lower_kernel, (first_spots, second_spots...]
    another operation x2, other arithmetic: 2.69 us -> 0.07 us  [gather_y_first(): held = jnp.stack(held)]
  transfers between devices with their start and end apart: 41 -> 40, of which waited for: 13 -> 14; matrix products, arithmetic and copies ran while one was open for 6% -> 2% of each run, Pallas kernels for 19% -> 20%
where the time goes in v2:
time: 221 us; the launch traced here: 220 us
  waiting for transfers between devices  94.5 us (43%)
  starting transfers between devices  60.8 us (28%)
  Pallas kernels  48.4 us (22%)
  local copies, waits for them, and re-layouts  11.6 us (5%)
  other arithmetic  2.71 us (1%)
    ppermute x15, waiting for transfers between devices, from_z(): return lax.ppermute(value, 'gy', pairs)  57.3 us
    ppermute x15, starting transfers between devices, from_z(): return lax.ppermute(value, 'gy', pairs)  44.9 us
    ppermute x14, waiting for transfers between devices, from_y(): return lax.ppermute(value, 'gy', pairs)  28.4 us
    pallas_call x2, Pallas kernels, per_device(): pl.pallas_call(functools.partial(attention_kernel, own_rows), grid=(1,),...  11.9 us
    ppermute x14, starting transfers between devices, from_y(): return lax.ppermute(value, 'gy', pairs)  9.68 us
    unnamed x76, local copies, waits for them, and re-layouts  9.06 us
    pallas_call x1, Pallas kernels, per_device(): pl.pallas_call(functools.partial(units_kernel, gated_spots, len(gated_arr...  8.75 us
    ppermute x4, waiting for transfers between devices, to_x(): return lax.ppermute(value, 'gx', pairs)  8.54 us
  transfers between devices with their start and end apart: 40, of which 14 were waited for; matrix products, arithmetic and copies ran while one was open for 2% of the time, Pallas kernels for 20%

profile of v2, /device:TPU:0, one launch (start us, length us, event | category | flops | bytes accessed | tf_op | source)
XLA Modules:
  0.0 219.8 jit_solution(13717079650095299200)
XLA Ops:
  0.7 5.1 %collective-permute-start.1 = (bf16[3,160,256]{2,1,0:T(8,128)(2,1)}, bf16[3,160,256]{2,1,0:T(8,128)(2,1)S(1)}, u32[]{:S(2)}, u32[]{:S(2)}) collective-permute-start(bf16[3,160,256]{2,1,0:T(8,128)(2,1)} %bitcast.37), channel_id=1, source_target_pairs={{0,6},{1,7},{2,0},{3,1},{4,2},{5,3},{6,4},{7,5},{8,14},{9,15},{10,... | collective-permute-start | bytes 737288 | tf_op jit(solution)/shard_map/ppermute | solution.py:42
  12.5 4.2 %collective-permute-start.3 = (bf16[3,160,256]{2,1,0:T(8,128)(2,1)S(1)}, bf16[3,160,256]{2,1,0:T(8,128)(2,1)}, u32[]{:S(2)}, u32[]{:S(2)}) collective-permute-start(bf16[3,160,256]{2,1,0:T(8,128)(2,1)S(1)} %collective-permute-done.1.rest_2_), channel_id=1, source_target_pairs={{0,6},{1,7},{2,0},{3,1},{4,2},{5,3},{6,4},{7,5},{8,14},{9,15},{10,... | collective-permute-start | bytes 737288 | tf_op jit(solution)/shard_map/ppermute | solution.py:42
  18.4 16.9 %collective-permute-done.3.rest_4_ = bf16[3,160,256]{2,1,0:T(8,128)(2,1)} collective-permute-done((bf16[3,160,256]{2,1,0:T(8,128)(2,1)S(1)}, bf16[3,160,256]{2,1,0:T(8,128)(2,1)}, u32[]{:S(2)}, u32[]{:S(2)}) %collective-permute-start.3) | collective-permute-done | bytes 245792 | tf_op jit(solution)/shard_map/ppermute | solution.py:42
  35.2 4.4 %collective-permute-start.5 = (bf16[3,160,256]{2,1,0:T(8,128)(2,1)}, bf16[3,160,256]{2,1,0:T(8,128)(2,1)}, u32[]{:S(2)}, u32[]{:S(2)}) collective-permute-start(bf16[3,160,256]{2,1,0:T(8,128)(2,1)} %collective-permute-done.3.rest_4_), channel_id=1, source_target_pairs={{0,6},{1,7},{2,0},{3,1},{4,2},{5,3},{6,4},{7,5},{8,14},{9,15},{10,... | collective-permute-start | bytes 737288 | tf_op jit(solution)/shard_map/ppermute | solution.py:42
  39.6 2.3 %collective-permute-start.12 = (bf16[2,160,256]{2,1,0:T(8,128)(2,1)S(1)}, bf16[2,160,256]{2,1,0:T(8,128)(2,1)}, u32[]{:S(2)}, u32[]{:S(2)}) collective-permute-start(bf16[2,160,256]{2,1,0:T(8,128)(2,1)S(1)} %collective-permute-done.11.refs_3_), channel_id=1, source_target_pairs={{0,6},{1,7},{2,0},{3,1},{4,2},{5,3},{6,4},{7,5},{8,14},{9,15},{10,... | collective-permute-start | bytes 491528 | tf_op jit(solution)/shard_map/ppermute | solution.py:42
  44.2 2.9 %collective-permute-done.12.refs_4_ = bf16[2,160,256]{2,1,0:T(8,128)(2,1)} collective-permute-done((bf16[2,160,256]{2,1,0:T(8,128)(2,1)S(1)}, bf16[2,160,256]{2,1,0:T(8,128)(2,1)}, u32[]{:S(2)}, u32[]{:S(2)}) %collective-permute-start.12) | collective-permute-done | bytes 163872 | tf_op jit(solution)/shard_map/ppermute | solution.py:42
  51.7 4.4 %collective-permute-start.13 = (bf16[2,160,256]{2,1,0:T(8,128)(2,1)}, bf16[2,160,256]{2,1,0:T(8,128)(2,1)}, u32[]{:S(2)}, u32[]{:S(2)}) collective-permute-start(bf16[2,160,256]{2,1,0:T(8,128)(2,1)} %collective-permute-done.12.refs_4_), channel_id=1, source_target_pairs={{0,6},{1,7},{2,0},{3,1},{4,2},{5,3},{6,4},{7,5},{8,14},{9,15},{10,... | collective-permute-start | bytes 491528 | tf_op jit(solution)/shard_map/ppermute | solution.py:42
  56.8 7.3 %stage.1.cycle_in = bf16[2,4608,256]{2,1,0:T(8,128)(2,1)} custom-call(bf16[2,4608,256]{2,1,0:T(8,128)(2,1)} %bitcast.28, s32[12]{0:T(128)} %stack.91.rest_0_.scalars, bf16[2,128,256]{2,1,0:T(8,128)(2,1)} %pad.4.rest_1_.sink_ref, f32[1,256]{1,0:T(1,128)} %bitcast.44, f32[2,1280]{1,0:T(2,128)} %pad_maximum_fusion.4.rest_3_.scale_ref, ...), custom_call_target="tpu_custom_call" | custom-call | tf_op jit(solution)/shard_map/stage/pallas_call | solution.py:471
  64.2 6.1 %qkv.1 = (bf16[512,256]{1,0:T(8,128)(2,1)}, bf16[2,4608,256]{2,1,0:T(8,128)(2,1)}) custom-call(s32[12]{0:T(128)} %stack.91.rest_0_.scalars, f32[1,256]{1,0:T(1,128)} %bitcast.45, bf16[2,4608,256]{2,1,0:T(8,128)(2,1)} %stage.1.cycle_in, bf16[3,160,256]{2,1,0:T(8,128)(2,1)} %bitcast.38, ...), custom_call_target="tpu_custom_call", output_to_operand_aliasing={{1}: (2, {})} | custom-call | tf_op jit(solution)/shard_map/qkv/pallas_call | solution.py:481
  70.3 5.9 %shard_map.150.refs_1_ = bf16[512,128]{1,0:T(8,128)(2,1)} custom-call(s32[12]{0:T(128)} %stack.91.rest_0_.scalars, bf16[512,256]{1,0:T(8,128)(2,1)} %get-tuple-element.10.query_ref, bf16[2,4608,256]{2,1,0:T(8,128)(2,1)} %get-tuple-element.11.cycle_ref, bf16[2,128,256]{2,1,0:T(8,128)(2,1)} %pad.4.rest_1_.sink_ref), custom_call_target="tpu_custom_call" | custom-call | tf_op jit(solution)/shard_map/pallas_call | solution.py:501
  76.2 6.0 %shard_map.149.refs_0_ = bf16[512,128]{1,0:T(8,128)(2,1)} custom-call(s32[12]{0:T(128)} %stack.91.rest_0_.scalars, bf16[512,256]{1,0:T(8,128)(2,1)} %get-tuple-element.10.query_ref, bf16[2,4608,256]{2,1,0:T(8,128)(2,1)} %get-tuple-element.11.cycle_ref, bf16[2,128,256]{2,1,0:T(8,128)(2,1)} %pad.4.rest_1_.sink_ref), custom_call_target="tpu_custom_call" | custom-call | tf_op jit(solution)/shard_map/pallas_call | solution.py:501
  82.2 2.9 %mix.1 = (bf16[256,1280]{1,0:T(8,128)(2,1)}, bf16[256,1280]{1,0:T(8,128)(2,1)}) custom-call(s32[12]{0:T(128)} %stack.91.rest_0_.scalars, bf16[512,128]{1,0:T(8,128)(2,1)} %shard_map.149.refs_0_, bf16[512,128]{1,0:T(8,128)(2,1)} %shard_map.150.refs_1_, bf16[2,160,256]{2,1,0:T(8,128)(2,1)} %copy-done.22, bf16[2,160,256]{2,1,0:T(8,128)(2,1)} %copy-done.31, ...), custom_call_target="tpu_custom_call" | custom-call | tf_op jit(solution)/shard_map/mix/pallas_call | solution.py:528
  86.2 8.9 %collective-permute-start.31 = (bf16[160,640]{1,0:T(8,128)(2,1)S(1)}, bf16[160,640]{1,0:T(8,128)(2,1)S(1)}, u32[]{:S(2)}, u32[]{:S(2)}) collective-permute-start(bf16[160,640]{1,0:T(8,128)(2,1)S(1)} %get-tuple-element.20.refs_4_), channel_id=1, source_target_pairs={{0,6},{1,7},{2,0},{3,1},{4,2},{5,3},{6,4},{7,5},{8,14},{9,15},{10,... | collective-permute-start | bytes 614408 | tf_op jit(solution)/shard_map/ppermute | solution.py:42
  95.1 7.0 %collective-permute-done.31.refs_6_ = bf16[160,640]{1,0:T(8,128)(2,1)S(1)} collective-permute-done((bf16[160,640]{1,0:T(8,128)(2,1)S(1)}, bf16[160,640]{1,0:T(8,128)(2,1)S(1)}, u32[]{:S(2)}, u32[]{:S(2)}) %collective-permute-start.31) | collective-permute-done | bytes 204832 | tf_op jit(solution)/shard_map/ppermute | solution.py:42
  102.1 2.2 collective-permute-start.33
  105.0 5.1 %collective-permute-done.33.refs_8_ = bf16[160,640]{1,0:T(8,128)(2,1)S(1)} collective-permute-done((bf16[160,640]{1,0:T(8,128)(2,1)S(1)}, bf16[160,640]{1,0:T(8,128)(2,1)S(1)}, u32[]{:S(2)}, u32[]{:S(2)}) %collective-permute-start.33) | collective-permute-done | bytes 204832 | tf_op jit(solution)/shard_map/ppermute | solution.py:42
  110.1 4.0 %collective-permute-start.35 = (bf16[160,640]{1,0:T(8,128)(2,1)S(1)}, bf16[160,640]{1,0:T(8,128)(2,1)S(1)}, u32[]{:S(2)}, u32[]{:S(2)}) collective-permute-start(bf16[160,640]{1,0:T(8,128)(2,1)S(1)} %collective-permute-done.33.refs_8_), channel_id=1, source_target_pairs={{0,6},{1,7},{2,0},{3,1},{4,2},{5,3},{6,4},{7,5},{8,14},{9,15},{10,... | collective-permute-start | bytes 614408 | tf_op jit(solution)/shard_map/ppermute | solution.py:42
  116.2 7.0 %collective-permute-done.35.refs_10_ = bf16[160,640]{1,0:T(8,128)(2,1)S(1)} collective-permute-done((bf16[160,640]{1,0:T(8,128)(2,1)S(1)}, bf16[160,640]{1,0:T(8,128)(2,1)S(1)}, u32[]{:S(2)}, u32[]{:S(2)}) %collective-permute-start.35) | collective-permute-done | bytes 204832 | tf_op jit(solution)/shard_map/ppermute | solution.py:42
  126.9 12.9 %collective-permute-done.21.refs_6_ = bf16[2,160,1280]{2,1,0:T(8,128)(2,1)} collective-permute-done((bf16[2,160,1280]{2,1,0:T(8,128)(2,1)}, bf16[2,160,1280]{2,1,0:T(8,128)(2,1)}, u32[]{:S(2)}, u32[]{:S(2)}) %collective-permute-start.21) | collective-permute-done | bytes 819232 | tf_op jit(solution)/shard_map/ppermute | solution.py:42
  140.5 3.7 %collective-permute-start.28 = (bf16[2,160,640]{2,1,0:T(8,128)(2,1)}, bf16[2,160,640]{2,1,0:T(8,128)(2,1)}, u32[]{:S(2)}, u32[]{:S(2)}) collective-permute-start(bf16[2,160,640]{2,1,0:T(8,128)(2,1)} %collective-permute-done.27.refs_1_), channel_id=1, source_target_pairs={{0,6},{1,7},{2,0},{3,1},{4,2},{5,3},{6,4},{7,5},{8,14},{9,15},{10,... | collective-permute-start | bytes 1228808 | tf_op jit(solution)/shard_map/ppermute | solution.py:42
  144.2 2.3 %shard_map.152.refs_10_ = bf16[128,1280]{1,0:T(8,128)(2,1)} custom-call(bf16[128,1280]{1,0:T(8,128)(2,1)} %collective-permute-done.8.rest_10_.base_ref, f32[2,1280]{1,0:T(2,128)} %pad_maximum_fusion.3.rest_4_.alpha_ref, bf16[128,1280]{1,0:T(8,128)(2,1)} %copy-done.21, bf16[128,1280]{1,0:T(8,128)(2,1)} %copy-done.25), custom_call_target="tpu_custom_call" | custom-call | tf_op jit(solution)/shard_map/pallas_call | solution.py:546
  146.5 2.3 %shard_map.151.refs_8_.base_ref = bf16[128,1280]{1,0:T(8,128)(2,1)} custom-call(bf16[128,1280]{1,0:T(8,128)(2,1)} %bitcast.30, f32[2,1280]{1,0:T(2,128)} %pad_maximum_fusion.3.rest_4_.alpha_ref, bf16[128,1280]{1,0:T(8,128)(2,1)} %copy-done.20, bf16[128,1280]{1,0:T(8,128)(2,1)} %copy-done.26), custom_call_target="tpu_custom_call" | custom-call | tf_op jit(solution)/shard_map/pallas_call | solution.py:546
  148.8 3.4 %collective-permute-done.28.refs_2_ = bf16[2,160,640]{2,1,0:T(8,128)(2,1)} collective-permute-done((bf16[2,160,640]{2,1,0:T(8,128)(2,1)}, bf16[2,160,640]{2,1,0:T(8,128)(2,1)}, u32[]{:S(2)}, u32[]{:S(2)}) %collective-permute-start.28) | collective-permute-done | bytes 409632 | tf_op jit(solution)/shard_map/ppermute | solution.py:42
  152.2 4.3 %collective-permute-start.29 = (bf16[2,160,640]{2,1,0:T(8,128)(2,1)}, bf16[2,160,640]{2,1,0:T(8,128)(2,1)}, u32[]{:S(2)}, u32[]{:S(2)}) collective-permute-start(bf16[2,160,640]{2,1,0:T(8,128)(2,1)} %collective-permute-done.28.refs_2_), channel_id=1, source_target_pairs={{0,6},{1,7},{2,0},{3,1},{4,2},{5,3},{6,4},{7,5},{8,14},{9,15},{10,... | collective-permute-start | bytes 1228808 | tf_op jit(solution)/shard_map/ppermute | solution.py:42
  158.5 5.2 %collective-permute-done.20.refs_5_ = bf16[2,160,1280]{2,1,0:T(8,128)(2,1)} collective-permute-done((bf16[2,160,1280]{2,1,0:T(8,128)(2,1)}, bf16[2,160,1280]{2,1,0:T(8,128)(2,1)}, u32[]{:S(2)}, u32[]{:S(2)}) %collective-permute-start.20) | collective-permute-done | bytes 819232 | tf_op jit(solution)/shard_map/ppermute | solution.py:50
  163.7 17.6 %collective-permute-done.22.refs_7_ = bf16[2,160,1280]{2,1,0:T(8,128)(2,1)} collective-permute-done((bf16[2,160,1280]{2,1,0:T(8,128)(2,1)}, bf16[2,160,1280]{2,1,0:T(8,128)(2,1)}, u32[]{:S(2)}, u32[]{:S(2)}) %collective-permute-start.22) | collective-permute-done | bytes 819232 | tf_op jit(solution)/shard_map/ppermute | solution.py:50
  181.3 8.8 %units.1.active_ref = bf16[512,1280]{1,0:T(8,128)(2,1)} custom-call(s32[12]{0:T(128)} %stack.91.rest_0_.scalars, f32[2,1280]{1,0:T(2,128)} %pad_maximum_fusion.4.rest_3_.scale_ref, bf16[2,160,1280]{2,1,0:T(8,128)(2,1)} %copy-done.18, bf16[2,160,1280]{2,1,0:T(8,128)(2,1)} %collective-permute-done.16.refs_1_, ...), custom_call_target="tpu_custom_call" | custom-call | tf_op jit(solution)/shard_map/units/pallas_call | solution.py:562
  190.1 3.3 %collective-permute-done.34.refs_9_ = bf16[160,640]{1,0:T(8,128)(2,1)} collective-permute-done((bf16[160,640]{1,0:T(8,128)(2,1)}, bf16[160,640]{1,0:T(8,128)(2,1)}, u32[]{:S(2)}, u32[]{:S(2)}) %collective-permute-start.34) | collective-permute-done | bytes 204832 | tf_op jit(solution)/shard_map/ppermute | solution.py:50
  193.4 2.2 collective-permute-done.36.refs_11_
  202.3 3.0 %shard_map.154 = (bf16[128,1280]{1,0:T(8,128)(2,1)S(1)}, bf16[128,1280]{1,0:T(8,128)(2,1)S(1)}) custom-call(s32[12]{0:T(128)S(1)} %copy-done.17, bf16[512,1280]{1,0:T(8,128)(2,1)S(1)} %copy-done, bf16[2,160,640]{2,1,0:T(8,128)(2,1)S(1)} %copy-done.2, bf16[2,160,640]{2,1,0:T(8,128)(2,1)} %collective-permute-done.27.refs_1_, ...), custom_call_target="tpu_custom_call" | custom-call | tf_op jit(solution)/shard_map/pallas_call | solution.py:581
  205.4 2.8 %shard_map.153 = (bf16[128,1280]{1,0:T(8,128)(2,1)S(1)}, bf16[128,1280]{1,0:T(8,128)(2,1)S(1)}) custom-call(s32[12]{0:T(128)S(1)} %copy-done.17, bf16[512,1280]{1,0:T(8,128)(2,1)S(1)} %copy-done, bf16[2,160,640]{2,1,0:T(8,128)(2,1)S(1)} %copy-done.2, bf16[2,160,640]{2,1,0:T(8,128)(2,1)} %collective-permute-done.27.refs_1_, ...), custom_call_target="tpu_custom_call" | custom-call | tf_op jit(solution)/shard_map/pallas_call | solution.py:581
  210.1 8.5 %collective-permute-done.39.refs_2_ = bf16[128,1280]{1,0:T(8,128)(2,1)S(1)} collective-permute-done((bf16[128,1280]{1,0:T(8,128)(2,1)S(1)}, bf16[128,1280]{1,0:T(8,128)(2,1)S(1)}, u32[]{:S(2)}, u32[]{:S(2)}) %collective-permute-start.39) | collective-permute-done | bytes 327712 | tf_op jit(solution)/shard_map/ppermute | solution.py:56
  (150 shorter events, 35.3 us)
Async XLA Ops:
  0.7 11.8 %collective-permute-start.1 = (bf16[3,160,256]{2,1,0:T(8,128)(2,1)}, bf16[3,160,256]{2,1,0:T(8,128)(2,1)S(1)}, u32[]{:S(2)}, u32[]{:S(2)}) collective-permute-start(bf16[3,160,256]{2,1,0:T(8,128)(2,1)} %bitcast.37), channel_id=1, source_target_pairs={{0,6},{1,7},{2,0},{3,1},{4,2},{5,3},{6,4},{7,5},{8,14},{9,15},{10,... | collective-permute-start | bytes 737288 | tf_op jit(solution)/shard_map/ppermute | solution.py:42
  8.0 48.2 %collective-permute-start.17 = (bf16[2,160,1280]{2,1,0:T(8,128)(2,1)S(1)}, bf16[2,160,1280]{2,1,0:T(8,128)(2,1)}, u32[]{:S(2)}, u32[]{:S(2)}) collective-permute-start(bf16[2,160,1280]{2,1,0:T(8,128)(2,1)S(1)} %pad_maximum_fusion.refs_0_), channel_id=1, source_target_pairs={{0,6},{1,7},{2,0},{3,1},{4,2},{5,3},{6,4},{7,5},{8,14},{9,15},{10,... | collective-permute-start | bytes 2457608 | tf_op jit(solution)/shard_map/ppermute | solution.py:42
  8.4 9.8 %collective-permute-start = (bf16[3,160,256]{2,1,0:T(8,128)(2,1)S(1)}, bf16[3,160,256]{2,1,0:T(8,128)(2,1)S(1)}, u32[]{:S(2)}, u32[]{:S(2)}) collective-permute-start(bf16[3,160,256]{2,1,0:T(8,128)(2,1)S(1)} %bitcast.39), channel_id=1, source_target_pairs={{0,1},{1,0},{2,3},{3,2},{4,5},{5,4},{6,7},{7,6},{8,9},{9,8},{10,11... | collective-permute-start | bytes 737288 | tf_op jit(solution)/shard_map/ppermute | solution.py:50
  12.5 22.7 %collective-permute-start.3 = (bf16[3,160,256]{2,1,0:T(8,128)(2,1)S(1)}, bf16[3,160,256]{2,1,0:T(8,128)(2,1)}, u32[]{:S(2)}, u32[]{:S(2)}) collective-permute-start(bf16[3,160,256]{2,1,0:T(8,128)(2,1)S(1)} %collective-permute-done.1.rest_2_), channel_id=1, source_target_pairs={{0,6},{1,7},{2,0},{3,1},{4,2},{5,3},{6,4},{7,5},{8,14},{9,15},{10,... | collective-permute-start | bytes 737288 | tf_op jit(solution)/shard_map/ppermute | solution.py:42
  16.7 25.2 %collective-permute-start.8 = (bf16[128,1280]{1,0:T(8,128)(2,1)S(1)}, bf16[128,1280]{1,0:T(8,128)(2,1)}, u32[]{:S(2)}, u32[]{:S(2)}) collective-permute-start(bf16[128,1280]{1,0:T(8,128)(2,1)S(1)} %bitcast.31), channel_id=1, source_target_pairs={{0,16},{8,24},{16,0},{24,8},{1,17},{9,25},{17,1},{25,9},{2,18},{10... | collective-permute-start | bytes 983048 | tf_op jit(solution)/shard_map/ppermute | solution.py:56
  18.2 25.3 %collective-permute-start.7 = (bf16[128,1280]{1,0:T(8,128)(2,1)S(1)}, bf16[128,1280]{1,0:T(8,128)(2,1)S(1)}, u32[]{:S(2)}, u32[]{:S(2)}) collective-permute-start(bf16[128,1280]{1,0:T(8,128)(2,1)S(1)} %bitcast.32), channel_id=1, source_target_pairs={{0,8},{8,0},{16,24},{24,16},{1,9},{9,1},{17,25},{25,17},{2,10},{10... | collective-permute-start | bytes 983048 | tf_op jit(solution)/shard_map/ppermute | solution.py:60
  18.2 21.4 %collective-permute-start.11 = (bf16[2,160,256]{2,1,0:T(8,128)(2,1)S(1)}, bf16[2,160,256]{2,1,0:T(8,128)(2,1)S(1)}, u32[]{:S(2)}, u32[]{:S(2)}) collective-permute-start(bf16[2,160,256]{2,1,0:T(8,128)(2,1)S(1)} %pad_maximum_fusion.2.refs_2_), channel_id=1, source_target_pairs={{0,6},{1,7},{2,0},{3,1},{4,2},{5,3},{6,4},{7,5},{8,14},{9,15},{10,... | collective-permute-start | bytes 491528 | tf_op jit(solution)/shard_map/ppermute | solution.py:42
  35.2 13.3 %collective-permute-start.5 = (bf16[3,160,256]{2,1,0:T(8,128)(2,1)}, bf16[3,160,256]{2,1,0:T(8,128)(2,1)}, u32[]{:S(2)}, u32[]{:S(2)}) collective-permute-start(bf16[3,160,256]{2,1,0:T(8,128)(2,1)} %collective-permute-done.3.rest_4_), channel_id=1, source_target_pairs={{0,6},{1,7},{2,0},{3,1},{4,2},{5,3},{6,4},{7,5},{8,14},{9,15},{10,... | collective-permute-start | bytes 737288 | tf_op jit(solution)/shard_map/ppermute | solution.py:42
  41.9 9.8 %collective-permute-start.2 = (bf16[3,160,256]{2,1,0:T(8,128)(2,1)S(1)}, bf16[3,160,256]{2,1,0:T(8,128)(2,1)S(1)}, u32[]{:S(2)}, u32[]{:S(2)}) collective-permute-start(bf16[3,160,256]{2,1,0:T(8,128)(2,1)S(1)} %collective-permute-done.1.rest_2_), channel_id=1, source_target_pairs={{0,1},{1,0},{2,3},{3,2},{4,5},{5,4},{6,7},{7,6},{8,9},{9,8},{10,11... | collective-permute-start | bytes 737288 | tf_op jit(solution)/shard_map/ppermute | solution.py:50
  43.5 20.7 %collective-permute-start.9 = (bf16[128,1280]{1,0:T(8,128)(2,1)}, bf16[128,1280]{1,0:T(8,128)(2,1)}, u32[]{:S(2)}, u32[]{:S(2)}) collective-permute-start(bf16[128,1280]{1,0:T(8,128)(2,1)} %collective-permute-done.8.rest_10_.base_ref), channel_id=1, source_target_pairs={{0,8},{8,0},{16,24},{24,16},{1,9},{9,1},{17,25},{25,17},{2,10},{10... | collective-permute-start | bytes 983048 | tf_op jit(solution)/shard_map/ppermute | solution.py:60
  47.0 17.1 %collective-permute-start.4 = (bf16[3,160,256]{2,1,0:T(8,128)(2,1)}, bf16[3,160,256]{2,1,0:T(8,128)(2,1)}, u32[]{:S(2)}, u32[]{:S(2)}) collective-permute-start(bf16[3,160,256]{2,1,0:T(8,128)(2,1)} %collective-permute-done.3.rest_4_), channel_id=1, source_target_pairs={{0,1},{1,0},{2,3},{3,2},{4,5},{5,4},{6,7},{7,6},{8,9},{9,8},{10,11... | collective-permute-start | bytes 737288 | tf_op jit(solution)/shard_map/ppermute | solution.py:50
  48.6 15.6 %collective-permute-start.6 = (bf16[3,160,256]{2,1,0:T(8,128)(2,1)}, bf16[3,160,256]{2,1,0:T(8,128)(2,1)}, u32[]{:S(2)}, u32[]{:S(2)}) collective-permute-start(bf16[3,160,256]{2,1,0:T(8,128)(2,1)} %collective-permute-done.5.rest_6_), channel_id=1, source_target_pairs={{0,1},{1,0},{2,3},{3,2},{4,5},{5,4},{6,7},{7,6},{8,9},{9,8},{10,11... | collective-permute-start | bytes 737288 | tf_op jit(solution)/shard_map/ppermute | solution.py:50
  51.7 30.4 %collective-permute-start.13 = (bf16[2,160,256]{2,1,0:T(8,128)(2,1)}, bf16[2,160,256]{2,1,0:T(8,128)(2,1)}, u32[]{:S(2)}, u32[]{:S(2)}) collective-permute-start(bf16[2,160,256]{2,1,0:T(8,128)(2,1)} %collective-permute-done.12.refs_4_), channel_id=1, source_target_pairs={{0,6},{1,7},{2,0},{3,1},{4,2},{5,3},{6,4},{7,5},{8,14},{9,15},{10,... | collective-permute-start | bytes 491528 | tf_op jit(solution)/shard_map/ppermute | solution.py:42
  56.1 57.9 %collective-permute-start.19 = (bf16[2,160,1280]{2,1,0:T(8,128)(2,1)}, bf16[2,160,1280]{2,1,0:T(8,128)(2,1)}, u32[]{:S(2)}, u32[]{:S(2)}) collective-permute-start(bf16[2,160,1280]{2,1,0:T(8,128)(2,1)} %collective-permute-done.17.refs_2_), channel_id=1, source_target_pairs={{0,6},{1,7},{2,0},{3,1},{4,2},{5,3},{6,4},{7,5},{8,14},{9,15},{10,... | collective-permute-start | bytes 2457608 | tf_op jit(solution)/shard_map/ppermute | solution.py:42
  85.1 29.3 %collective-permute-start.14 = (bf16[256,1280]{1,0:T(8,128)(2,1)}, bf16[256,1280]{1,0:T(8,128)(2,1)S(1)}, u32[]{:S(2)}, u32[]{:S(2)}) collective-permute-start(bf16[256,1280]{1,0:T(8,128)(2,1)} %get-tuple-element.13), channel_id=1, source_target_pairs={{0,8},{8,0},{16,24},{24,16},{1,9},{9,1},{17,25},{25,17},{2,10},{10... | collective-permute-start | bytes 1966088 | tf_op jit(solution)/shard_map/ppermute | solution.py:60
  86.2 15.9 %collective-permute-start.31 = (bf16[160,640]{1,0:T(8,128)(2,1)S(1)}, bf16[160,640]{1,0:T(8,128)(2,1)S(1)}, u32[]{:S(2)}, u32[]{:S(2)}) collective-permute-start(bf16[160,640]{1,0:T(8,128)(2,1)S(1)} %get-tuple-element.20.refs_4_), channel_id=1, source_target_pairs={{0,6},{1,7},{2,0},{3,1},{4,2},{5,3},{6,4},{7,5},{8,14},{9,15},{10,... | collective-permute-start | bytes 614408 | tf_op jit(solution)/shard_map/ppermute | solution.py:42
  104.3 44.5 %collective-permute-start.16 = (bf16[2,160,1280]{2,1,0:T(8,128)(2,1)}, bf16[2,160,1280]{2,1,0:T(8,128)(2,1)}, u32[]{:S(2)}, u32[]{:S(2)}) collective-permute-start(bf16[2,160,1280]{2,1,0:T(8,128)(2,1)} %copy-done.18), channel_id=1, source_target_pairs={{0,1},{1,0},{2,3},{3,2},{4,5},{5,4},{6,7},{7,6},{8,9},{9,8},{10,11... | collective-permute-start | bytes 2457608 | tf_op jit(solution)/shard_map/ppermute | solution.py:50
  104.4 20.3 %collective-permute-start.27 = (bf16[2,160,640]{2,1,0:T(8,128)(2,1)S(1)}, bf16[2,160,640]{2,1,0:T(8,128)(2,1)}, u32[]{:S(2)}, u32[]{:S(2)}) collective-permute-start(bf16[2,160,640]{2,1,0:T(8,128)(2,1)S(1)} %pad_maximum_fusion.1.refs_0_), channel_id=1, source_target_pairs={{0,6},{1,7},{2,0},{3,1},{4,2},{5,3},{6,4},{7,5},{8,14},{9,15},{10,... | collective-permute-start | bytes 1228808 | tf_op jit(solution)/shard_map/ppermute | solution.py:42
  110.1 13.2 %collective-permute-start.35 = (bf16[160,640]{1,0:T(8,128)(2,1)S(1)}, bf16[160,640]{1,0:T(8,128)(2,1)S(1)}, u32[]{:S(2)}, u32[]{:S(2)}) collective-permute-start(bf16[160,640]{1,0:T(8,128)(2,1)S(1)} %collective-permute-done.33.refs_8_), channel_id=1, source_target_pairs={{0,6},{1,7},{2,0},{3,1},{4,2},{5,3},{6,4},{7,5},{8,14},{9,15},{10,... | collective-permute-start | bytes 614408 | tf_op jit(solution)/shard_map/ppermute | solution.py:42
  114.1 25.7 %collective-permute-start.21 = (bf16[2,160,1280]{2,1,0:T(8,128)(2,1)}, bf16[2,160,1280]{2,1,0:T(8,128)(2,1)}, u32[]{:S(2)}, u32[]{:S(2)}) collective-permute-start(bf16[2,160,1280]{2,1,0:T(8,128)(2,1)} %collective-permute-done.19.refs_4_), channel_id=1, source_target_pairs={{0,6},{1,7},{2,0},{3,1},{4,2},{5,3},{6,4},{7,5},{8,14},{9,15},{10,... | collective-permute-start | bytes 2457608 | tf_op jit(solution)/shard_map/ppermute | solution.py:42
  114.7 10.1 %collective-permute-start.24 = (bf16[128,1280]{1,0:T(8,128)(2,1)S(1)}, bf16[128,1280]{1,0:T(8,128)(2,1)S(1)}, u32[]{:S(2)}, u32[]{:S(2)}) collective-permute-start(bf16[128,1280]{1,0:T(8,128)(2,1)S(1)} %get-tuple-element.19.refs_0_), channel_id=1, source_target_pairs={{0,16},{8,24},{16,0},{24,8},{1,17},{9,25},{17,1},{25,9},{2,18},{10... | collective-permute-start | bytes 983048 | tf_op jit(solution)/shard_map/ppermute | solution.py:56
  123.3 16.6 %collective-permute-start.15 = (bf16[128,1280]{1,0:T(8,128)(2,1)S(1)}, bf16[128,1280]{1,0:T(8,128)(2,1)S(1)}, u32[]{:S(2)}, u32[]{:S(2)}) collective-permute-start(bf16[128,1280]{1,0:T(8,128)(2,1)S(1)} %get-tuple-element.18.refs_0_), channel_id=1, source_target_pairs={{0,16},{8,24},{16,0},{24,8},{1,17},{9,25},{17,1},{25,9},{2,18},{10... | collective-permute-start | bytes 983048 | tf_op jit(solution)/shard_map/ppermute | solution.py:56
  124.7 27.4 %collective-permute-start.18 = (bf16[2,160,1280]{2,1,0:T(8,128)(2,1)}, bf16[2,160,1280]{2,1,0:T(8,128)(2,1)}, u32[]{:S(2)}, u32[]{:S(2)}) collective-permute-start(bf16[2,160,1280]{2,1,0:T(8,128)(2,1)} %collective-permute-done.17.refs_2_), channel_id=1, source_target_pairs={{0,1},{1,0},{2,3},{3,2},{4,5},{5,4},{6,7},{7,6},{8,9},{9,8},{10,11... | collective-permute-start | bytes 2457608 | tf_op jit(solution)/shard_map/ppermute | solution.py:50
  124.8 38.9 %collective-permute-start.20 = (bf16[2,160,1280]{2,1,0:T(8,128)(2,1)}, bf16[2,160,1280]{2,1,0:T(8,128)(2,1)}, u32[]{:S(2)}, u32[]{:S(2)}) collective-permute-start(bf16[2,160,1280]{2,1,0:T(8,128)(2,1)} %collective-permute-done.19.refs_4_), channel_id=1, source_target_pairs={{0,1},{1,0},{2,3},{3,2},{4,5},{5,4},{6,7},{7,6},{8,9},{9,8},{10,11... | collective-permute-start | bytes 2457608 | tf_op jit(solution)/shard_map/ppermute | solution.py:50
  139.8 41.5 %collective-permute-start.22 = (bf16[2,160,1280]{2,1,0:T(8,128)(2,1)}, bf16[2,160,1280]{2,1,0:T(8,128)(2,1)}, u32[]{:S(2)}, u32[]{:S(2)}) collective-permute-start(bf16[2,160,1280]{2,1,0:T(8,128)(2,1)} %collective-permute-done.21.refs_6_), channel_id=1, source_target_pairs={{0,1},{1,0},{2,3},{3,2},{4,5},{5,4},{6,7},{7,6},{8,9},{9,8},{10,11... | collective-permute-start | bytes 2457608 | tf_op jit(solution)/shard_map/ppermute | solution.py:50
  140.5 11.6 %collective-permute-start.28 = (bf16[2,160,640]{2,1,0:T(8,128)(2,1)}, bf16[2,160,640]{2,1,0:T(8,128)(2,1)}, u32[]{:S(2)}, u32[]{:S(2)}) collective-permute-start(bf16[2,160,640]{2,1,0:T(8,128)(2,1)} %collective-permute-done.27.refs_1_), channel_id=1, source_target_pairs={{0,6},{1,7},{2,0},{3,1},{4,2},{5,3},{6,4},{7,5},{8,14},{9,15},{10,... | collective-permute-start | bytes 1228808 | tf_op jit(solution)/shard_map/ppermute | solution.py:42
  152.2 43.4 %collective-permute-start.29 = (bf16[2,160,640]{2,1,0:T(8,128)(2,1)}, bf16[2,160,640]{2,1,0:T(8,128)(2,1)}, u32[]{:S(2)}, u32[]{:S(2)}) collective-permute-start(bf16[2,160,640]{2,1,0:T(8,128)(2,1)} %collective-permute-done.28.refs_2_), channel_id=1, source_target_pairs={{0,6},{1,7},{2,0},{3,1},{4,2},{5,3},{6,4},{7,5},{8,14},{9,15},{10,... | collective-permute-start | bytes 1228808 | tf_op jit(solution)/shard_map/ppermute | solution.py:42
  156.5 33.6 %collective-permute-start.30 = (bf16[160,640]{1,0:T(8,128)(2,1)}, bf16[160,640]{1,0:T(8,128)(2,1)}, u32[]{:S(2)}, u32[]{:S(2)}) collective-permute-start(bf16[160,640]{1,0:T(8,128)(2,1)} %copy-done.4), channel_id=1, source_target_pairs={{0,1},{1,0},{2,3},{3,2},{4,5},{5,4},{6,7},{7,6},{8,9},{9,8},{10,11... | collective-permute-start | bytes 614408 | tf_op jit(solution)/shard_map/ppermute | solution.py:50
  158.2 31.9 %collective-permute-start.32 = (bf16[160,640]{1,0:T(8,128)(2,1)}, bf16[160,640]{1,0:T(8,128)(2,1)}, u32[]{:S(2)}, u32[]{:S(2)}) collective-permute-start(bf16[160,640]{1,0:T(8,128)(2,1)} %copy-done.7), channel_id=1, source_target_pairs={{0,1},{1,0},{2,3},{3,2},{4,5},{5,4},{6,7},{7,6},{8,9},{9,8},{10,11... | collective-permute-start | bytes 614408 | tf_op jit(solution)/shard_map/ppermute | solution.py:50
  163.7 29.7 %collective-permute-start.34 = (bf16[160,640]{1,0:T(8,128)(2,1)}, bf16[160,640]{1,0:T(8,128)(2,1)}, u32[]{:S(2)}, u32[]{:S(2)}) collective-permute-start(bf16[160,640]{1,0:T(8,128)(2,1)} %copy-done.10), channel_id=1, source_target_pairs={{0,1},{1,0},{2,3},{3,2},{4,5},{5,4},{6,7},{7,6},{8,9},{9,8},{10,11... | collective-permute-start | bytes 614408 | tf_op jit(solution)/shard_map/ppermute | solution.py:50
  181.3 14.3 %collective-permute-start.36 = (bf16[160,640]{1,0:T(8,128)(2,1)}, bf16[160,640]{1,0:T(8,128)(2,1)}, u32[]{:S(2)}, u32[]{:S(2)}) collective-permute-start(bf16[160,640]{1,0:T(8,128)(2,1)} %copy-done.13), channel_id=1, source_target_pairs={{0,1},{1,0},{2,3},{3,2},{4,5},{5,4},{6,7},{7,6},{8,9},{9,8},{10,11... | collective-permute-start | bytes 614408 | tf_op jit(solution)/shard_map/ppermute | solution.py:50
  209.0 9.7 %collective-permute-start.39 = (bf16[128,1280]{1,0:T(8,128)(2,1)S(1)}, bf16[128,1280]{1,0:T(8,128)(2,1)S(1)}, u32[]{:S(2)}, u32[]{:S(2)}) collective-permute-start(bf16[128,1280]{1,0:T(8,128)(2,1)S(1)} %add_convert_fusion.1), channel_id=1, source_target_pairs={{0,16},{8,24},{16,0},{24,8},{1,17},{9,25},{17,1},{25,9},{2,18},{10... | collective-permute-start | bytes 983048 | tf_op jit(solution)/shard_map/ppermute | solution.py:56
  (46 other events, 580.1 us)
